TPU v7x, 256 devices: a whole 4x4x8 slice. The times are simulated.
256 devices in a mesh: samp: 8 (over z), feat: 32 (over y, x, core).
Axes of the slice: x: 4, y: 4, z: 8, core: 2. Of those that a mesh axis runs over, the one named last changes fastest.
Arguments:
- data: bfloat16 [32768, 512], P('samp'), may hold values from -6 to 6
- omega: bfloat16 [512, 24576], P(None, 'feat'), may hold values from -0.25 to 0.25
- phase: float32 [24576], P('feat'), may hold values from -3.140625 to 3.140625
- earlier: bfloat16 [24576, 12288], P('feat', 'samp'), may hold values from -3 to 3, as said below
- ridge: float32 [1], replicated, may hold values from 0.5 to 2
Outputs:
- factor: float32 [24576, 512], P('feat')
Inputs may be any that keep to these rules, and one draw needn't show every extreme that they name: The spectral norm of earlier[:512] is at most 0.56, so that shifted[:512] is positive definite.
All inputs are finite; a program needn't handle non-finite values.
Results may differ from a plain program's by a relative error of at most 0.015.
Values may be sent and summed in bfloat16 or wider, within the bound.
No kernel may reach another device: no remote copies, remote signals or barrier semaphores. Data moves between devices by JAX's collectives and lax.ppermute only.
A program may use at most 128 MiB of HBM per device.

v0:
```python
import jax
import jax.numpy as jnp
from jax import lax
from jax.sharding import PartitionSpec as P

PANEL = 512


def from_root(value, axis, source):
    kept = jnp.where(lax.axis_index(axis) == source, value, 0).astype(value.dtype)
    return lax.psum(kept, axis)


def on_device(data, omega, phase, earlier, ridge):
    samples_all = data.shape[0] * lax.axis_size("samp")
    scale = jnp.sqrt(jnp.float32(2.0) / samples_all)
    proj = jnp.dot(data, omega, preferred_element_type=jnp.float32) + phase[None, :]
    local_feat = (scale * jnp.cos(proj)).astype(jnp.bfloat16)
    panel_feat = from_root(local_feat[:, :PANEL], "feat", 0)
    panel_rows = from_root(earlier[:PANEL], "feat", 0)
    partial_value = lax.dot_general(
        local_feat, panel_feat, (((0,), (0,)), ((), ())), preferred_element_type=jnp.float32
    )
    partial_value = partial_value - lax.dot_general(
        earlier, panel_rows, (((1,), (1,)), ((), ())), preferred_element_type=jnp.float32
    )
    feat_index = lax.axis_index("feat")
    local_rows = omega.shape[1]
    summed = lax.psum(partial_value, "samp")
    first = feat_index * local_rows
    shift_value = ridge[0]
    row_ids = first + jnp.arange(summed.shape[0], dtype=jnp.int32)
    col_ids = jnp.arange(PANEL, dtype=jnp.int32)
    summed = summed + shift_value * (row_ids[:, None] == col_ids[None, :]).astype(jnp.float32)
    diag_block = from_root(summed[:PANEL], "feat", 0)
    lower = jnp.linalg.cholesky(diag_block)
    solved = lax.linalg.triangular_solve(
        lower, summed, left_side=False, lower=True, transpose_a=True
    )
    return solved


def solution(mesh):
    in_specs = (P("samp", None), P(None, "feat"), P("feat"), P("feat", "samp"), P())
    out_specs = P("feat", None)
    return jax.shard_map(
        on_device, mesh=mesh, in_specs=in_specs, out_specs=out_specs, check_vma=False
    )
```

profile of v0, /device:TPU:1, one launch (start us, length us, event | category | flops | bytes accessed | tf_op | source)
XLA Modules:
  0.0 569.2 jit_solution(12703660423301359845)
XLA Ops:
  6.5 1.1 copy-done
  7.7 45.1 %multiply_convert_fusion = bf16[4096,768]{1,0:T(8,128)(2,1)S(1)} fusion(bf16[4096,512]{1,0:T(8,128)(2,1)} %param.5, bf16[512,768]{1,0:T(8,128)(2,1)S(1)} %copy-done, f32[768]{0:T(1024)} %param.7), kind=kOutput, calls=%fused_computation.2 | convolution fusion | flops 3230662656 | bytes 11275264 | tf_op jit(solution)/shard_map/dot_general | solution.py:17
  52.8 2.4 slice_select_fusion
  55.1 1.8 copy-done.2
  57.0 1.2 slice_select_fusion.1
  58.3 128.6 %all-reduce.10.cloned.1.call-done = (bf16[4096,512]{1,0:T(8,128)(2,1)}, bf16[512,1536]{1,0:T(8,128)(2,1)}) async-done(((bf16[4096,512]{1,0:T(8,128)(2,1)}, bf16[512,1536]{1,0:T(8,128)(2,1)}), (bf16[4096,512]{1,0:T(8,128)(2,1)}, bf16[512,1536]{1,0:T(8,128)(2,1)})) %all-reduce.10.cloned.1.call-update) | async-done | bytes 5767184 | tf_op jit(solution)/shard_map/psum | solution.py:11
  186.8 7.3 %fusion.31 = f32[768,512]{0,1:T(8,128)S(1)} fusion(bf16[4096,768]{1,0:T(8,128)(2,1)} %copy-done.2, bf16[4096,512]{1,0:T(8,128)(2,1)} %get-tuple-element.25), kind=kOutput, calls=%fused_computation.75 | convolution fusion | flops 3221225472 | bytes 12058624 | tf_op jit(solution)/shard_map/dot_general | solution.py:21
  194.1 2.6 bitcast_subtract_fusion
  197.6 73.7 %all-reduce.6.cloned.1.call-done = f32[768,512]{0,1:T(8,128)} async-done(((f32[768,512]{0,1:T(8,128)}), f32[768,512]{0,1:T(8,128)}) %all-reduce.6.cloned.1.call-update) | async-done | bytes 1572880 | tf_op jit(solution)/shard_map/psum | solution.py:29
  271.3 1.6 select_add_fusion
  272.9 1.1 slice_select_fusion.2
  274.6 118.4 %all-reduce.8.cloned.1.call-done = f32[512,512]{0,1:T(8,128)} async-done(((f32[512,512]{0,1:T(8,128)}), f32[512,512]{0,1:T(8,128)}) %all-reduce.8.cloned.1.call-update) | async-done | bytes 1048592 | tf_op jit(solution)/shard_map/psum | solution.py:11
  393.1 2.6 copy.7
  395.7 1.4 fusion.5
  397.2 1.0 copy-done.3
  398.1 11.7 %cholesky.103 = f32[128,128]{1,0:T(8,128)S(1)} custom-call(f32[128,128]{1,0:T(8,128)S(1)} %cholesky.263), custom_call_target="Cholesky" | custom-call | tf_op jit(solution)/shard_map/jit(cholesky)/cholesky | solution.py:36
  409.9 9.8 %custom-call.30 = f32[1,128,128]{1,2,0:T(8,128)S(1)} custom-call(f32[1,128,128]{2,1,0:T(8,128)S(1)} %get-tuple-element.34), custom_call_target="InvertDiagBlocksLowerTriangular" | custom-call | tf_op jit(solution)/shard_map/jit(cholesky)/cholesky | solution.py:36
  419.7 1.2 fusion.14
  420.9 1.3 convolution_subtract_fusion.3
  422.2 0.7 copy-done.6
  422.9 11.7 %cholesky.215 = f32[128,128]{1,0:T(8,128)S(1)} custom-call(f32[128,128]{1,0:T(8,128)S(1)} %cholesky.267), custom_call_target="Cholesky" | custom-call | tf_op jit(solution)/shard_map/jit(cholesky)/cholesky | solution.py:36
  434.7 0.8 copy.9
  435.6 10.6 %custom-call.31 = f32[1,128,128]{1,2,0:T(8,128)} custom-call(f32[1,128,128]{2,1,0:T(8,128)S(1)} %get-tuple-element.32), custom_call_target="InvertDiagBlocksLowerTriangular" | custom-call | tf_op jit(solution)/shard_map/jit(cholesky)/cholesky | solution.py:36
  446.4 0.9 constant_dynamic-update-slice_fusion.3
  447.7 1.5 convolution_subtract_fusion.4
  449.8 13.2 %cholesky.236 = f32[128,128]{1,0:T(8,128)} custom-call(f32[128,128]{1,0:T(8,128)} %cholesky.272), custom_call_target="Cholesky" | custom-call | tf_op jit(solution)/shard_map/jit(cholesky)/cholesky | solution.py:36
  463.0 1.5 select_reduce_fusion.1
  464.5 1.6 copy.12
  466.0 0.8 constant_dynamic-update-slice_fusion
  466.9 11.3 %custom-call.32 = f32[1,128,128]{1,2,0:T(8,128)} custom-call(f32[1,128,128]{2,1,0:T(8,128)} %get-tuple-element.30), custom_call_target="InvertDiagBlocksLowerTriangular" | custom-call | tf_op jit(solution)/shard_map/jit(cholesky)/cholesky | solution.py:36
  478.1 1.1 convolution_dynamic-update-slice_fusion.1
  479.3 1.3 convolution_subtract_fusion.5
  480.6 11.9 %cholesky.253 = f32[128,128]{1,0:T(8,128)S(1)} custom-call(f32[128,128]{1,0:T(8,128)S(1)} %convolution_subtract_fusion.5), custom_call_target="Cholesky" | custom-call | tf_op jit(solution)/shard_map/jit(cholesky)/cholesky | solution.py:36
  492.7 0.7 compare_reduce_fusion.1
  494.0 0.7 compare_reduce_fusion.2
  497.2 1.1 select_select_fusion
  498.3 0.6 triangular_solve.90
  499.0 14.5 %while.1 = (s32[]{:T(128)}, f32[512,512]{0,1:T(8,128)}, s32[4,2]{0,1:T(2,128)S(1)}, f32[4,128,128]{2,1,0:T(8,128)}, s32[]{:T(128)}) while((s32[]{:T(128)}, f32[512,512]{0,1:T(8,128)}, s32[4,2]{0,1:T(2,128)S(1)}, f32[4,128,128]{2,1,0:T(8,128)}, s32[]{:T(128)}) %tuple.24), condition=%wide.while_cond, body=%wide.while_body.sunk | while | flops 2 | bytes 393829 | solution.py:37
  499.7 2.2 dynamic-slice.7
  503.3 2.2 dynamic-slice.7
  507.0 2.2 dynamic-slice.7
  509.3 0.6 bitcast_dynamic-update-slice_fusion.2
  510.6 2.2 dynamic-slice.7
  513.5 40.1 %custom-call.33 = f32[4,128,128]{1,2,0:T(8,128)S(1)} custom-call(f32[4,128,128]{2,1,0:T(8,128)} %get-tuple-element.12), custom_call_target="InvertDiagBlocksLowerTriangular" | custom-call | tf_op jit(solution)/shard_map/triangular_solve | solution.py:37
  554.2 1.4 convolution_subtract_fusion.1
  556.1 1.5 convolution_subtract_fusion.2
  558.1 1.9 convolution_subtract_fusion
  560.7 1.6 copy.16
  (59 shorter events, 10.1 us)
Async XLA Ops:
  6.5 1.1 copy-start
  6.5 180.3 %all-reduce.10.cloned.1.call-start = ((), (), s32[]{:S(2)}) async-start(), calls=%async_computation.2 | async-start | bytes 11534336 | tf_op jit(solution)/shard_map/psum | solution.py:11
  52.7 4.2 copy-start.2
  52.8 4.2 copy-start.4
  58.2 213.1 %all-reduce.6.cloned.1.call-start = ((), (), s32[]{:S(2)}) async-start(), calls=%async_computation | async-start | bytes 3145728 | tf_op jit(solution)/shard_map/psum | solution.py:29
  186.8 7.3 %copy-start.5 = (bf16[768,1536]{1,0:T(8,128)(2,1)S(1)}, bf16[768,1536]{1,0:T(8,128)(2,1)}, u32[]{:S(2)}) copy-start(bf16[768,1536]{1,0:T(8,128)(2,1)} %param.8) | copy-start | bytes 7077892
  186.8 7.3 %copy-start.9 = (bf16[512,1536]{1,0:T(8,128)(2,1)S(1)}, bf16[512,1536]{1,0:T(8,128)(2,1)}, u32[]{:S(2)}) copy-start(bf16[512,1536]{1,0:T(8,128)(2,1)} %get-tuple-element.26) | copy-start | bytes 4718596
  196.8 196.3 %all-reduce.8.cloned.1.call-start = ((), (), s32[]{:S(2)}) async-start(), calls=%async_computation.1 | async-start | bytes 2097152 | tf_op jit(solution)/shard_map/psum | solution.py:11
  393.1 2.6 copy-start.1
  397.1 1.0 copy-start.3
  422.2 0.7 copy-start.6
  446.3 1.1 copy-start.7
  446.3 1.1 copy-start.8
Sparse Core Ops, SparseCore 0:
  58.4 128.4 all-reduce.9
  196.9 74.4 all-reduce.5
  274.6 118.4 all-reduce.7
where the time goes:
time: 575 us; the launch traced here: 569 us
  waiting for transfers between devices  321 us (56%)
  other arithmetic  133 us (23%)
  matrix products  68.5 us (12%)
  local copies, waits for them, and re-layouts  29.2 us (5%)
  between operations  17 us (3%)
    psum x2, waiting for transfers between devices, from_root(): return lax.psum(kept, axis)  247 us
    another operation x14, other arithmetic, on_device(): lower = jnp.linalg.cholesky(diag_block)  83.8 us
    psum x1, waiting for transfers between devices, on_device(): summed = lax.psum(partial_value, 'samp')  73.7 us
    dot_general x1, matrix products, on_device(): jnp.dot(data, omega, preferred_element_type=jnp.float32) + phase[None, :]  45.1 us
    another operation x4, other arithmetic, on_device(): lax.linalg.triangular_solve(lower, summed, left_side=False, lower=True, t...  41.9 us
    another operation x20, local copies, waits for them, and re-layouts  14.5 us
  transfers between devices with their start and end apart: 3, of which 3 were waited for; matrix products, arithmetic and copies ran while one was open for 0% of the time, Pallas kernels for 0%

commit v1 on v0

v1 whole, which is shorter than its diff:
```python
import functools
import math

import jax
import jax.numpy as jnp
import numpy as np
from jax import lax
from jax.experimental import pallas as pl
from jax.experimental.pallas import tpu as pltpu
from jax.sharding import PartitionSpec as P

PANEL = 512
SIDE = 4
EXTRA = 16
HIGHEST = lax.Precision.HIGHEST
NT = (((1,), (1,)), ((), ()))
TN = (((0,), (0,)), ((), ()))
INV_TURN = 1.0 / (2.0 * math.pi)
MAGIC = 12582912.0


def sine_coefficients():
    u = np.cos(np.pi * (np.arange(4000) + 0.5) / 4000) * 0.25
    fit = np.polynomial.chebyshev.Chebyshev.fit(u * u, -np.sin(2 * np.pi * u) / u, 4, domain=[0, 1 / 16])
    poly = fit.convert(kind=np.polynomial.Polynomial, domain=[-1, 1], window=[-1, 1])
    return [float(v) for v in poly.coef]


SINE = sine_coefficients()


def scaled_cos(turns, scale):
    r = turns - ((turns + MAGIC) - MAGIC)
    u = jnp.abs(r) - 0.25
    s = u * u
    coefs = [v * scale for v in SINE]
    p = coefs[4]
    for v in coefs[3::-1]:
        p = p * s + v
    return p * u


def local_kernel(w_ref, ph_ref, x_ref, o_ref, *, scale):
    proj = lax.dot_general(w_ref[...], x_ref[...], NT, preferred_element_type=jnp.float32)
    o_ref[...] = scaled_cos(proj * INV_TURN + ph_ref[...], scale).astype(jnp.bfloat16)


def local_features(wt, ph, data, scale, bs=1024):
    rows, din = wt.shape
    samples = data.shape[0]
    return pl.pallas_call(
        functools.partial(local_kernel, scale=scale),
        grid=(samples // bs,),
        in_specs=[
            pl.BlockSpec((rows, din), lambda i: (0, 0)),
            pl.BlockSpec((rows, 1), lambda i: (0, 0)),
            pl.BlockSpec((bs, din), lambda i: (i, 0)),
        ],
        out_specs=pl.BlockSpec((rows, bs), lambda i: (0, i)),
        out_shape=jax.ShapeDtypeStruct((rows, samples), jnp.bfloat16),
        cost_estimate=pl.CostEstimate(flops=2 * rows * samples * din, bytes_accessed=12 << 20, transcendentals=0),
        name="local_features",
    )(wt, ph, data)


def gram_kernel(pos_ref, v_ref, x_ref, f_ref, e_ref, s_ref, d_ref, ph_ref, phd_ref, *, scale):
    i = pl.program_id(0)
    y, x, c, row = pos_ref[0], pos_ref[1], pos_ref[2], pos_ref[3]

    def piece(p):
        half, q = p // SIDE, p % SIDE
        return (c, lax.rem(x - q + SIDE, SIDE)) if half == 0 else (1 - c, lax.rem(y - q + SIDE, SIDE))

    def rows_of(p):
        a, b = piece(p)
        return v_ref[a, b, :256, :]

    def row_slice(p):
        a, b = piece(p)
        return v_ref[a, b, pl.ds(pl.multiple_of(lax.rem(row, 256), 16), 16), :]

    def sixteen(p):
        return jnp.where(row < 256, row_slice(p).astype(jnp.float32), row_slice(p + 1).astype(jnp.float32)).astype(jnp.bfloat16)

    @pl.when(i == 0)
    def _():
        a, b = piece(0)
        tail = v_ref[a, b, 256:256 + EXTRA, :].astype(jnp.float32)
        ph = (tail[0:1] + tail[1:2]) + tail[2:3]
        ph_ref[...] = ph
        hit = lax.broadcasted_iota(jnp.int32, (16, PANEL), 1) == row + lax.broadcasted_iota(jnp.int32, (16, PANEL), 0)
        phd_ref[...] = jnp.sum(jnp.where(hit, jnp.broadcast_to(ph, (16, PANEL)), 0.0), axis=1, keepdims=True)
        s_ref[...] = jnp.zeros_like(s_ref)
        d_ref[...] = jnp.zeros_like(d_ref)

    for chunk in range(3):
        @pl.when(i == chunk)
        def _(chunk=chunk):
            for h in range(2):
                panel = rows_of(2 + 2 * chunk + h)
                cols = slice(256 * h, 256 * h + 256)
                s_ref[:, cols] -= lax.dot_general(e_ref[...], panel, NT, preferred_element_type=jnp.float32)
                d_ref[:, cols] -= lax.dot_general(sixteen(2 + 2 * chunk), panel, NT, preferred_element_type=jnp.float32)

    data = x_ref[...]
    panel_feat = []
    for h in range(2):
        proj = lax.dot_general(data, rows_of(h), NT, preferred_element_type=jnp.float32)
        panel_feat.append(scaled_cos(proj * INV_TURN + ph_ref[:, 256 * h:256 * h + 256], scale).astype(jnp.bfloat16))
    proj = lax.dot_general(sixteen(0), data, NT, preferred_element_type=jnp.float32)
    feat = scaled_cos(proj * INV_TURN + phd_ref[...], scale).astype(jnp.bfloat16)
    for h in range(2):
        cols = slice(256 * h, 256 * h + 256)
        s_ref[:, cols] += jnp.dot(f_ref[...], panel_feat[h], preferred_element_type=jnp.float32)
        d_ref[:, cols] += jnp.dot(feat, panel_feat[h], preferred_element_type=jnp.float32)


def gram(pos, v, data, feat, earlier, scale, bs=512):
    rows, samples = feat.shape
    din = data.shape[1]
    return pl.pallas_call(
        functools.partial(gram_kernel, scale=scale),
        grid=(samples // bs,),
        in_specs=[
            pl.BlockSpec(memory_space=pltpu.SMEM),
            pl.BlockSpec(v.shape, lambda i: (0, 0, 0, 0)),
            pl.BlockSpec((bs, din), lambda i: (i, 0)),
            pl.BlockSpec((rows, bs), lambda i: (0, i)),
            pl.BlockSpec((rows, PANEL), lambda i: (0, jnp.minimum(i, 2))),
        ],
        out_specs=[pl.BlockSpec((rows, PANEL), lambda i: (0, 0)), pl.BlockSpec((16, PANEL), lambda i: (0, 0))],
        out_shape=[
            jax.ShapeDtypeStruct((rows, PANEL), jnp.float32),
            jax.ShapeDtypeStruct((16, PANEL), jnp.float32),
        ],
        scratch_shapes=[pltpu.VMEM((1, PANEL), jnp.float32), pltpu.VMEM((16, 1), jnp.float32)],
        cost_estimate=pl.CostEstimate(flops=8 << 30, bytes_accessed=16 << 20, transcendentals=0),
        name="gram",
    )(pos, v, data, feat, earlier)


def split2(v):
    high = v.astype(jnp.bfloat16)
    return high, (v - high.astype(jnp.float32)).astype(jnp.bfloat16)


def split3(v):
    high = v.astype(jnp.bfloat16)
    rest = v - high.astype(jnp.float32)
    mid = rest.astype(jnp.bfloat16)
    return high, mid, (rest - mid.astype(jnp.float32)).astype(jnp.bfloat16)


def block_inverse(n_ref, lb_ref):
    sub = lax.broadcasted_iota(jnp.int32, (8, 128), 0)
    lane = lax.broadcasted_iota(jnp.int32, (8, 128), 1)

    def step(s, carry):
        k = pl.multiple_of(s * 8, 8)
        rows = n_ref[pl.ds(k, 8), :]
        pivot = pltpu.roll(rows[:, :128], jnp.where(s == 0, 0, 128 - k), 1)
        a = [[None] * 8 for _ in range(8)]
        for j in range(8):
            col = jnp.broadcast_to(pivot[:, j:j + 1], (8, 128))
            for i in range(j, 8):
                a[i][j] = jnp.broadcast_to(col[i:i + 1, :], (8, 128))
        low = [[None] * 8 for _ in range(8)]
        root = []
        for j in range(8):
            inverse = 1.0 / a[j][j]
            root.append(lax.rsqrt(a[j][j]))
            for i in range(j + 1, 8):
                low[i][j] = a[i][j] * inverse
            for i in range(j + 1, 8):
                for m in range(j + 1, i + 1):
                    a[i][m] = a[i][m] - low[i][j] * a[m][j]
        t = [[None] * 8 for _ in range(8)]
        for j in range(8):
            for i in range(j + 1, 8):
                acc = low[i][j]
                for m in range(j + 1, i):
                    acc = acc + low[i][m] * t[m][j]
                t[i][j] = -acc
        w0 = jnp.zeros((8, 128), jnp.float32)
        w1 = jnp.zeros((8, 128), jnp.float32)
        for j in range(8):
            col = jnp.where(sub == j, root[j], 0.0)
            for i in range(j + 1, 8):
                col = jnp.where(sub == i, root[i] * t[i][j], col)
            w0 = w0 + col * jnp.broadcast_to(rows[j:j + 1, :128], (8, 128))
            w1 = w1 + col * jnp.broadcast_to(rows[j:j + 1, 128:], (8, 128))
        lb_ref[pl.ds(k, 8), :] = w1
        gh, gm, gl = split3(jnp.where(lane >= k + 8, w0, 0.0))
        wh, wm, wl = split3(jnp.concatenate([w0, w1], axis=1))
        left = jnp.concatenate([gh, gh, gm, gh, gm, gl], axis=0)
        right = jnp.concatenate([wh, wm, wh, wl, wm, wh], axis=0)
        n_ref[...] -= lax.dot_general(left, right, TN, preferred_element_type=jnp.float32)
        return carry

    lax.fori_loop(0, 16, step, 0)


def factor_kernel(ridge_ref, d_ref, out_ref, m_ref, j_ref, n_ref, lb_ref):
    n = PANEL
    eye = lax.broadcasted_iota(jnp.int32, (n, n), 0) == lax.broadcasted_iota(jnp.int32, (n, n), 1)
    m_ref[...] = d_ref[...].reshape(n, n) + jnp.where(eye, ridge_ref[0], 0.0)
    j_ref[...] = jnp.where(eye, 1.0, 0.0)
    out_ref[...] = jnp.zeros((n, n), jnp.float32)
    small = lax.broadcasted_iota(jnp.int32, (128, 128), 0) == lax.broadcasted_iota(jnp.int32, (128, 128), 1)
    for b in range(n // 128):
        r0, r1 = 128 * b, 128 * b + 128
        n_ref[:, :128] = m_ref[r0:r1, r0:r1]
        n_ref[:, 128:] = jnp.where(small, 1.0, 0.0)
        block_inverse(n_ref, lb_ref)
        lb = lb_ref[...]
        jb = jnp.dot(lb, j_ref[r0:r1, :r1], precision=HIGHEST, preferred_element_type=jnp.float32)
        out_ref[r0:r1, :r1] = jb
        if r1 < n:
            r = jnp.dot(lb, m_ref[r0:r1, r1:], precision=HIGHEST, preferred_element_type=jnp.float32)
            m_ref[r1:, r1:] -= lax.dot_general(r, r, TN, precision=HIGHEST, preferred_element_type=jnp.float32)
            j_ref[r1:, :r1] -= lax.dot_general(r, jb, TN, precision=HIGHEST, preferred_element_type=jnp.float32)


def factor_inverse(ridge, d):
    n = PANEL
    return pl.pallas_call(
        factor_kernel,
        out_shape=jax.ShapeDtypeStruct((n, n), jnp.float32),
        in_specs=[pl.BlockSpec(memory_space=pltpu.SMEM), pl.BlockSpec(memory_space=pltpu.VMEM)],
        out_specs=pl.BlockSpec(memory_space=pltpu.VMEM),
        scratch_shapes=[
            pltpu.VMEM((n, n), jnp.float32),
            pltpu.VMEM((n, n), jnp.float32),
            pltpu.VMEM((128, 256), jnp.float32),
            pltpu.VMEM((128, 128), jnp.float32),
        ],
        cost_estimate=pl.CostEstimate(flops=8 << 30, bytes_accessed=2 << 20, transcendentals=0),
        name="factor_inverse",
    )(ridge, d)


def solve_kernel(pos_ref, ridge_ref, s_ref, inv_ref, o_ref):
    rows = s_ref.shape[0]
    row_ids = pos_ref[4] + lax.broadcasted_iota(jnp.int32, (rows, PANEL), 0)
    hit = row_ids == lax.broadcasted_iota(jnp.int32, (rows, PANEL), 1)
    sh, sl = split2(s_ref[...] + jnp.where(hit, ridge_ref[0], 0.0))
    for b in range(PANEL // 256):
        r0, r1 = 256 * b, 256 * b + 256
        lh, ll = split2(inv_ref[r0:r1, :r1])
        out = lax.dot_general(sh[:, :r1], ll, NT, preferred_element_type=jnp.float32)
        out += lax.dot_general(sl[:, :r1], lh, NT, preferred_element_type=jnp.float32)
        o_ref[:, r0:r1] = out + lax.dot_general(sh[:, :r1], lh, NT, preferred_element_type=jnp.float32)


def solve(pos, ridge, s, inverse, bs=256):
    rows = s.shape[0]
    smem = pl.BlockSpec(memory_space=pltpu.SMEM)
    return pl.pallas_call(
        solve_kernel,
        out_shape=jax.ShapeDtypeStruct(s.shape, jnp.float32),
        in_specs=[smem, smem, pl.BlockSpec(memory_space=pltpu.VMEM), pl.BlockSpec(memory_space=pltpu.VMEM)],
        out_specs=pl.BlockSpec(memory_space=pltpu.VMEM),
        cost_estimate=pl.CostEstimate(flops=6 * rows * PANEL * PANEL, bytes_accessed=4 << 20, transcendentals=0),
        name="solve",
    )(pos, ridge, s, inverse)


def feat_of(y, x, c):
    return ((y % SIDE) * SIDE + x % SIDE) * 2 + c


def share_panel(mine, partner, y, x, c):
    side = range(SIDE)

    def permute(value, pairs):
        return lax.ppermute(value, "feat", pairs)

    def first(value, received, has):
        total = received[0] + received[1] + received[2]
        return jnp.where(has, value, total)

    half = permute(partner, [(feat_of(0, 0, 0), feat_of(0, 0, 1))])
    half = jnp.where(c == 0, mine, half)
    got = [permute(half[k], [(feat_of(0, 0, 0), feat_of(0, k, 0)), (feat_of(0, 0, 1), feat_of(k, 0, 1))]) for k in (1, 2, 3)]
    held = first(half[0], got, (x == 0) & (y == 0))
    got = [
        permute(
            held,
            [(feat_of(0, j, 0), feat_of(k, j, 0)) for j in side] + [(feat_of(j, 0, 1), feat_of(j, k, 1)) for j in side],
        )
        for k in (1, 2, 3)
    ]
    held = first(held, got, jnp.where(c == 0, y, x) == 0)
    got = [
        permute(
            held,
            [(feat_of(i, j, 0), feat_of(i, j + k, 0)) for i in side for j in side]
            + [(feat_of(i, j, 1), feat_of(i + k, j, 1)) for i in side for j in side],
        )
        for k in (1, 2, 3)
    ]
    own = jnp.stack([held, *got])
    other = permute(own, [(i, i ^ 1) for i in range(2 * SIDE * SIDE)])
    return jnp.stack([own, other])


def on_device(data, omega, phase, earlier, ridge):
    samples_all = data.shape[0] * lax.axis_size("samp")
    scale = math.sqrt(2.0 / samples_all)
    feat = lax.axis_index("feat")
    rows = omega.shape[1]
    c = feat % 2
    x = (feat // 2) % SIDE
    y = feat // (2 * SIDE)
    pos = jnp.stack([y, x, c, feat * 16, feat * rows]).astype(jnp.int32)

    weights = omega.T
    turns = phase * INV_TURN
    high = lax.reduce_precision(turns, 8, 7)
    mid = lax.reduce_precision(turns - high, 8, 7)
    low = turns - high - mid
    tail = jnp.stack([high[:PANEL], mid[:PANEL], low[:PANEL]]).astype(jnp.bfloat16)
    tail = jnp.concatenate([tail, jnp.zeros((EXTRA - 3, PANEL), jnp.bfloat16)])

    def with_tail(blocks):
        return jnp.stack([jnp.concatenate([b, tail]) for b in blocks])

    def panel_rows(k):
        return [earlier[256 * h:256 * h + 256, PANEL * k:PANEL * k + PANEL] for h in range(2)]

    mine = with_tail([weights[:256], weights[256:512], *panel_rows(0)])
    partner = with_tail([*panel_rows(1), *panel_rows(2)])
    v = share_panel(mine, partner, y, x, c)

    local = local_features(weights, turns[:, None], data, scale)
    s, d = gram(pos, v, data, local, earlier, scale)
    summed = lax.psum(s, "samp")
    d = lax.all_to_all(jnp.broadcast_to(d, (8, 16, PANEL)), "samp", 0, 0).sum(0)
    d = lax.all_to_all(jnp.broadcast_to(d, (32, 16, PANEL)), "feat", 0, 0)
    inverse = factor_inverse(ridge, d)
    return solve(pos, ridge, summed, inverse)


def solution(mesh):
    in_specs = (P("samp", None), P(None, "feat"), P("feat"), P("feat", "samp"), P())
    out_specs = P("feat", None)
    return jax.shard_map(
        on_device, mesh=mesh, in_specs=in_specs, out_specs=out_specs, check_vma=False
    )
```

time: 575 us -> 203 us (0.35)
  waiting for transfers between devices: 321 us -> 54.2 us
  other arithmetic: 133 us -> 4.78 us
  Pallas kernels: 0 us -> 69.9 us
  matrix products: 68.5 us -> 0 us
  starting transfers between devices: 0.26 us -> 27 us
  local copies, waits for them, and re-layouts: 29.2 us -> 10.2 us
  blocking collectives: 0 us -> 19 us
    psum x3 -> x1, waiting for transfers between devices: 321 us -> 21.6 us  [on_device(): summed = lax.psum(s, 'samp')]
    another operation x18 -> x3, other arithmetic: 126 us -> 1.95 us  [the longest x2 1.81 us: share_panel(): return jnp.stack([own, other])]
    pallas_call x0 -> x4, Pallas kernels: none -> 69.9 us  [the longest x1 34.8 us: factor_inverse(): pl.pallas_call(factor_kernel, out_shape=jax.ShapeDtypeStruct((n, n), jnp....]
    dot_general x3 -> x0, matrix products: 54.9 us -> none  [the longest x1 45.1 us: on_device(): jnp.dot(data, omega, preferred_element_type=jnp.float32) + phase[None, :]]
    another operation x35 -> x4, local copies, waits for them, and re-layouts: 21.9 us -> 0.67 us  [the longest x1 0.65 us: on_device(): pos = jnp.stack([y, x, c, feat * 16, feat * rows]).astype(jnp.int32)]
    all_to_all x0 -> x1, blocking collectives: none -> 19 us  [on_device(): d = lax.all_to_all(jnp.broadcast_to(d, (8, 16, PANEL)), 'samp', 0, 0).sum(0)]
    ppermute x0 -> x11, starting transfers between devices: none -> 18.1 us  [permute(): return lax.ppermute(value, 'feat', pairs)]
    ppermute x0 -> x11, waiting for transfers between devices: none -> 16.2 us  [permute(): return lax.ppermute(value, 'feat', pairs)]
  transfers between devices with their start and end apart: 3 -> 13, of which waited for: 3 -> 9; matrix products, arithmetic and copies ran while one was open for 0% -> 2% of each run, Pallas kernels for 0% -> 24%
where the time goes in v1:
time: 203 us; the launch traced here: 199 us
  Pallas kernels  69.9 us (34%)
  waiting for transfers between devices  54.2 us (27%)
  starting transfers between devices  27 us (13%)
  blocking collectives  19 us (9%)
  between operations  14.4 us (7%)
  local copies, waits for them, and re-layouts  10.2 us (5%)
  other arithmetic  4.78 us (2%)
    pallas_call x1, Pallas kernels, factor_inverse(): pl.pallas_call(factor_kernel, out_shape=jax.ShapeDtypeStruct((n, n), jnp....  34.8 us
    psum x1, waiting for transfers between devices, on_device(): summed = lax.psum(s, 'samp')  21.6 us
    all_to_all x1, blocking collectives, on_device(): d = lax.all_to_all(jnp.broadcast_to(d, (8, 16, PANEL)), 'samp', 0, 0).sum(0)  19 us
    pallas_call x1, Pallas kernels, gram(): pl.pallas_call(functools.partial(gram_kernel, scale=scale), grid=(samples...  18.4 us
    ppermute x11, starting transfers between devices, permute(): return lax.ppermute(value, 'feat', pairs)  18.1 us
    ppermute x11, waiting for transfers between devices, permute(): return lax.ppermute(value, 'feat', pairs)  16.2 us
    all_to_all x1, waiting for transfers between devices, on_device(): d = lax.all_to_all(jnp.broadcast_to(d, (32, 16, PANEL)), 'feat', 0, 0)  15.7 us
    pallas_call x1, Pallas kernels, local_features(): pl.pallas_call(functools.partial(local_kernel, scale=scale), grid=(sample...  12.6 us
  transfers between devices with their start and end apart: 13, of which 9 were waited for; matrix products, arithmetic and copies ran while one was open for 2% of the time, Pallas kernels for 24%

profile of v1, /device:TPU:1, one launch (start us, length us, event | category | flops | bytes accessed | tf_op | source)
XLA Modules:
  0.0 199.4 jit_solution(15753192464781834583)
XLA Ops:
  6.5 1.3 broadcast_multiply_fusion
  7.9 1.5 fusion.3
  9.4 0.3 concatenate.45
  9.7 0.3 concatenate.46
  10.0 0.3 concatenate.47
  10.2 0.3 concatenate.48
  10.5 0.1 pad_maximum_fusion.1
  10.7 1.3 collective-permute-start
  12.0 0.3 concatenate.43
  12.2 0.3 concatenate.44
  12.5 1.4 copy.9
  14.0 0.3 concatenate.41
  14.3 0.9 concatenate.42
  15.2 2.3 %collective-permute-done = bf16[4,272,512]{2,1,0:T(8,128)(2,1)} collective-permute-done((bf16[4,272,512]{2,1,0:T(8,128)(2,1)S(1)}, bf16[4,272,512]{2,1,0:T(8,128)(2,1)}, u32[]{:S(2)}, u32[]{:S(2)}) %collective-permute-start) | collective-permute-done | bytes 1114144 | tf_op jit(solution)/shard_map/ppermute | solution.py:276
  17.5 1.4 maximum_select_fusion
  18.9 0.1 slice_bitcast_fusion.1
  19.0 2.1 %collective-permute-start.1 = (bf16[272,512]{1,0:T(8,128)(2,1)S(1)}, bf16[272,512]{1,0:T(8,128)(2,1)S(1)}, u32[]{:S(2)}, u32[]{:S(2)}) collective-permute-start(bf16[272,512]{1,0:T(8,128)(2,1)S(1)} %get-tuple-element.19), channel_id=1, source_target_pairs={{0,2},{1,9},{32,34},{33,41},{64,66},{65,73},{96,98},{97,105},{128,... | collective-permute-start | bytes 835592 | tf_op jit(solution)/shard_map/ppermute | solution.py:276
  21.1 2.3 %collective-permute-start.2 = (bf16[272,512]{1,0:T(8,128)(2,1)S(1)}, bf16[272,512]{1,0:T(8,128)(2,1)S(1)}, u32[]{:S(2)}, u32[]{:S(2)}) collective-permute-start(bf16[272,512]{1,0:T(8,128)(2,1)S(1)} %get-tuple-element.17), channel_id=1, source_target_pairs={{0,4},{1,17},{32,36},{33,49},{64,68},{65,81},{96,100},{97,113},{12... | collective-permute-start | bytes 835592 | tf_op jit(solution)/shard_map/ppermute | solution.py:276
  23.4 1.3 collective-permute-start.3
  24.8 2.8 %collective-permute-done.2 = bf16[272,512]{1,0:T(8,128)(2,1)S(1)} collective-permute-done((bf16[272,512]{1,0:T(8,128)(2,1)S(1)}, bf16[272,512]{1,0:T(8,128)(2,1)S(1)}, u32[]{:S(2)}, u32[]{:S(2)}) %collective-permute-start.2) | collective-permute-done | bytes 278560 | tf_op jit(solution)/shard_map/ppermute | solution.py:276
  27.6 0.6 collective-permute-done.3
  28.3 1.3 collective-permute-start.4
  29.6 1.3 collective-permute-start.5
  30.9 1.3 collective-permute-start.6
  32.2 0.8 collective-permute-done.4
  33.0 3.0 %collective-permute-done.5 = bf16[272,512]{1,0:T(8,128)(2,1)S(1)} collective-permute-done((bf16[272,512]{1,0:T(8,128)(2,1)S(1)}, bf16[272,512]{1,0:T(8,128)(2,1)S(1)}, u32[]{:S(2)}, u32[]{:S(2)}) %collective-permute-start.5) | collective-permute-done | bytes 278560 | tf_op jit(solution)/shard_map/ppermute | solution.py:276
  36.1 0.1 collective-permute-start.7
  36.2 4.3 %collective-permute-start.8 = (bf16[272,512]{1,0:T(8,128)(2,1)S(1)}, bf16[272,512]{1,0:T(8,128)(2,1)S(1)}, u32[]{:S(2)}, u32[]{:S(2)}) collective-permute-start(bf16[272,512]{1,0:T(8,128)(2,1)S(1)} %add_select_fusion), channel_id=1, source_target_pairs={{0,4},{2,6},{4,0},{6,2},{8,12},{10,14},{12,8},{14,10},{16,20},{18,... | collective-permute-start | bytes 835592 | tf_op jit(solution)/shard_map/ppermute | solution.py:276
  40.5 0.6 collective-permute-start.9
  41.0 2.5 %collective-permute-done.7 = bf16[272,512]{1,0:T(8,128)(2,1)S(1)} collective-permute-done((bf16[272,512]{1,0:T(8,128)(2,1)S(1)}, bf16[272,512]{1,0:T(8,128)(2,1)S(1)}, u32[]{:S(2)}, u32[]{:S(2)}) %collective-permute-start.7) | collective-permute-done | bytes 278560 | tf_op jit(solution)/shard_map/ppermute | solution.py:276
  43.5 4.2 %collective-permute-done.8 = bf16[272,512]{1,0:T(8,128)(2,1)S(1)} collective-permute-done((bf16[272,512]{1,0:T(8,128)(2,1)S(1)}, bf16[272,512]{1,0:T(8,128)(2,1)S(1)}, u32[]{:S(2)}, u32[]{:S(2)}) %collective-permute-start.8) | collective-permute-done | bytes 278560 | tf_op jit(solution)/shard_map/ppermute | solution.py:276
  47.7 0.2 fusion.2
  47.9 2.2 %collective-permute-start.10 = (bf16[4,272,512]{2,1,0:T(8,128)(2,1)S(1)}, bf16[4,272,512]{2,1,0:T(8,128)(2,1)S(1)}, u32[]{:S(2)}, u32[]{:S(2)}) collective-permute-start(bf16[4,272,512]{2,1,0:T(8,128)(2,1)S(1)} %get-tuple-element.16), channel_id=1, source_target_pairs={{0,1},{1,0},{2,3},{3,2},{4,5},{5,4},{6,7},{7,6},{8,9},{9,8},{10,11... | collective-permute-start | bytes 3342344 | tf_op jit(solution)/shard_map/ppermute | solution.py:276
  50.1 0.9 broadcast_in_dim.16.ph_ref
  51.0 0.6 stack.91.pos_ref
  51.7 12.6 %local_features.1.f_ref = bf16[768,4096]{1,0:T(8,128)(2,1)} custom-call(bf16[768,512]{1,0:T(8,128)(2,1)} %bitcast.32, f32[768,1]{1,0:T(8,128)} %broadcast_in_dim.16.ph_ref, bf16[4096,512]{1,0:T(8,128)(2,1)} %x_ref.3), custom_call_target="tpu_custom_call" | custom-call | flops 3221225472 | bytes 12582912 | tf_op jit(solution)/shard_map/local_features/pallas_call | solution.py:51
  64.2 1.6 pad_maximum_fusion.v_ref
  65.9 18.4 %gram.1 = (f32[768,512]{1,0:T(8,128)}, f32[16,512]{1,0:T(8,128)}) custom-call(s32[5]{0:T(128)} %stack.91.pos_ref, bf16[2,4,272,512]{3,2,1,0:T(8,128)(2,1)} %pad_maximum_fusion.v_ref, bf16[4096,512]{1,0:T(8,128)(2,1)} %x_ref.3, bf16[768,4096]{1,0:T(8,128)(2,1)} %local_features.1.f_ref, bf16[768,1536]{1,0:T(8,128)(2,1)} %e_ref.1), custom_call_target="tpu_custom_call" | custom-call | flops 8589934592 | bytes 16777216 | tf_op jit(solution)/shard_map/gram/pallas_call | solution.py:121
  84.3 0.8 broadcast_in_dim.14
  85.1 19.0 %all_to_all.10 = f32[8,16,512]{2,1,0:T(8,128)S(1)} all-to-all(f32[8,16,512]{2,1,0:T(8,128)S(1)} %broadcast_in_dim.14), channel_id=1, replica_groups=mesh['samp'=8,'feat'=32] {'samp'}, dimensions={0} | all-to-all | bytes 524288 | tf_op jit(solution)/shard_map/all_to_all | solution.py:338
  104.1 1.1 broadcast_in_dim.15
  105.2 8.8 %all-to-all-start.1 = ((f32[32,16,512]{2,1,0:T(8,128)}), f32[32,16,512]{2,1,0:T(8,128)S(1)}, u32[]{:S(2)}, u32[]{:S(2)}) async-start(f32[32,16,512]{2,1,0:T(8,128)} %broadcast_in_dim.15), calls=%async_computation.1 | async-start | bytes 2097152 | tf_op jit(solution)/shard_map/all_to_all | solution.py:339
  114.1 0.7 all-reduce.2.cloned.1.call-update
  115.4 15.7 %all-to-all-done.1.d_ref = f32[32,16,512]{2,1,0:T(8,128)S(1)} async-done(((f32[32,16,512]{2,1,0:T(8,128)}), f32[32,16,512]{2,1,0:T(8,128)S(1)}, u32[]{:S(2)}, u32[]{:S(2)}) %all-to-all-start.1) | async-done | bytes 1048608 | tf_op jit(solution)/shard_map/all_to_all | solution.py:339
  131.1 1.0 copy-done.1
  132.1 34.8 %factor_inverse.1.inv_ref = f32[512,512]{1,0:T(8,128)} custom-call(f32[1]{0:T(128)S(6)} %copy.12.ridge_ref, f32[32,16,512]{2,1,0:T(8,128)} %copy-done.1), custom_call_target="tpu_custom_call" | custom-call | flops 8589934592 | bytes 2097152 | tf_op jit(solution)/shard_map/factor_inverse/pallas_call | solution.py:226
  166.9 21.6 %all-reduce.2.cloned.1.call-done.s_ref = f32[768,512]{1,0:T(8,128)} async-done(((f32[768,512]{1,0:T(8,128)}), f32[768,512]{1,0:T(8,128)}) %all-reduce.2.cloned.1.call-update) | async-done | bytes 1572880 | tf_op jit(solution)/shard_map/psum | solution.py:337
  188.5 4.1 %solve.1 = f32[768,512]{1,0:T(8,128)} custom-call(s32[5]{0:T(128)} %stack.91.pos_ref, f32[1]{0:T(128)S(6)} %copy.12.ridge_ref, f32[768,512]{1,0:T(8,128)} %all-reduce.2.cloned.1.call-done.s_ref, f32[512,512]{1,0:T(8,128)} %factor_inverse.1.inv_ref), custom_call_target="tpu_custom_call" | custom-call | flops 1207959552 | bytes 4194304 | tf_op jit(solution)/shard_map/solve/pallas_call | solution.py:258
  (27 shorter events, 0.3 us)
Async XLA Ops:
  7.8 6.1 %copy-start.2 = (bf16[1,512]{1,0:T(2,128)(2,1)}, bf16[1,512]{1,0:T(2,128)(2,1)S(1)}, u32[]{:S(2)}) copy-start(bf16[1,512]{1,0:T(2,128)(2,1)S(1)} %stack.92) | copy-start | bytes 3076
  7.8 6.1 %copy-start.3 = (bf16[1,512]{1,0:T(2,128)(2,1)}, bf16[1,512]{1,0:T(2,128)(2,1)S(1)}, u32[]{:S(2)}) copy-start(bf16[1,512]{1,0:T(2,128)(2,1)S(1)} %stack.93) | copy-start | bytes 3076
  7.9 6.1 %copy-start.4 = (bf16[1,512]{1,0:T(2,128)(2,1)}, bf16[1,512]{1,0:T(2,128)(2,1)S(1)}, u32[]{:S(2)}) copy-start(bf16[1,512]{1,0:T(2,128)(2,1)S(1)} %stack.94) | copy-start | bytes 3076
  10.7 6.9 %collective-permute-start = (bf16[4,272,512]{2,1,0:T(8,128)(2,1)S(1)}, bf16[4,272,512]{2,1,0:T(8,128)(2,1)}, u32[]{:S(2)}, u32[]{:S(2)}) collective-permute-start(bf16[4,272,512]{2,1,0:T(8,128)(2,1)S(1)} %pad_maximum_fusion.1), channel_id=1, source_target_pairs={{0,1},{32,33},{64,65},{96,97},{128,129},{160,161},{192,193},{224,2... | collective-permute-start | bytes 3342344 | tf_op jit(solution)/shard_map/ppermute | solution.py:276
  13.9 5.0 %copy-start = (bf16[512,768]{0,1:T(8,128)(2,1)}, bf16[512,768]{0,1:T(8,128)(2,1)S(1)}, u32[]{:S(2)}) copy-start(bf16[512,768]{0,1:T(8,128)(2,1)S(1)} %copy.9) | copy-start | bytes 2359300
  19.0 5.8 %collective-permute-start.1 = (bf16[272,512]{1,0:T(8,128)(2,1)S(1)}, bf16[272,512]{1,0:T(8,128)(2,1)S(1)}, u32[]{:S(2)}, u32[]{:S(2)}) collective-permute-start(bf16[272,512]{1,0:T(8,128)(2,1)S(1)} %get-tuple-element.19), channel_id=1, source_target_pairs={{0,2},{1,9},{32,34},{33,41},{64,66},{65,73},{96,98},{97,105},{128,... | collective-permute-start | bytes 835592 | tf_op jit(solution)/shard_map/ppermute | solution.py:276
  21.1 6.4 %collective-permute-start.2 = (bf16[272,512]{1,0:T(8,128)(2,1)S(1)}, bf16[272,512]{1,0:T(8,128)(2,1)S(1)}, u32[]{:S(2)}, u32[]{:S(2)}) collective-permute-start(bf16[272,512]{1,0:T(8,128)(2,1)S(1)} %get-tuple-element.17), channel_id=1, source_target_pairs={{0,4},{1,17},{32,36},{33,49},{64,68},{65,81},{96,100},{97,113},{12... | collective-permute-start | bytes 835592 | tf_op jit(solution)/shard_map/ppermute | solution.py:276
  23.4 4.8 %collective-permute-start.3 = (bf16[272,512]{1,0:T(8,128)(2,1)S(1)}, bf16[272,512]{1,0:T(8,128)(2,1)S(1)}, u32[]{:S(2)}, u32[]{:S(2)}) collective-permute-start(bf16[272,512]{1,0:T(8,128)(2,1)S(1)} %get-tuple-element.18), channel_id=1, source_target_pairs={{0,6},{1,25},{32,38},{33,57},{64,70},{65,89},{96,102},{97,121},{12... | collective-permute-start | bytes 835592 | tf_op jit(solution)/shard_map/ppermute | solution.py:276
  28.3 4.8 %collective-permute-start.4 = (bf16[272,512]{1,0:T(8,128)(2,1)S(1)}, bf16[272,512]{1,0:T(8,128)(2,1)S(1)}, u32[]{:S(2)}, u32[]{:S(2)}) collective-permute-start(bf16[272,512]{1,0:T(8,128)(2,1)S(1)} %fusion), channel_id=1, source_target_pairs={{0,8},{2,10},{4,12},{6,14},{1,3},{9,11},{17,19},{25,27},{32,40},{3... | collective-permute-start | bytes 835592 | tf_op jit(solution)/shard_map/ppermute | solution.py:276
  29.6 6.4 %collective-permute-start.5 = (bf16[272,512]{1,0:T(8,128)(2,1)S(1)}, bf16[272,512]{1,0:T(8,128)(2,1)S(1)}, u32[]{:S(2)}, u32[]{:S(2)}) collective-permute-start(bf16[272,512]{1,0:T(8,128)(2,1)S(1)} %fusion), channel_id=1, source_target_pairs={{0,16},{2,18},{4,20},{6,22},{1,5},{9,13},{17,21},{25,29},{32,48},{... | collective-permute-start | bytes 835592 | tf_op jit(solution)/shard_map/ppermute | solution.py:276
  30.9 5.1 %collective-permute-start.6 = (bf16[272,512]{1,0:T(8,128)(2,1)S(1)}, bf16[272,512]{1,0:T(8,128)(2,1)S(1)}, u32[]{:S(2)}, u32[]{:S(2)}) collective-permute-start(bf16[272,512]{1,0:T(8,128)(2,1)S(1)} %fusion), channel_id=1, source_target_pairs={{0,24},{2,26},{4,28},{6,30},{1,7},{9,15},{17,23},{25,31},{32,56},{... | collective-permute-start | bytes 835592 | tf_op jit(solution)/shard_map/ppermute | solution.py:276
  36.1 7.4 %collective-permute-start.7 = (bf16[272,512]{1,0:T(8,128)(2,1)S(1)}, bf16[272,512]{1,0:T(8,128)(2,1)S(1)}, u32[]{:S(2)}, u32[]{:S(2)}) collective-permute-start(bf16[272,512]{1,0:T(8,128)(2,1)S(1)} %add_select_fusion), channel_id=1, source_target_pairs={{0,2},{2,4},{4,6},{6,0},{8,10},{10,12},{12,14},{14,8},{16,18},{18,... | collective-permute-start | bytes 835592 | tf_op jit(solution)/shard_map/ppermute | solution.py:276
  36.2 11.5 %collective-permute-start.8 = (bf16[272,512]{1,0:T(8,128)(2,1)S(1)}, bf16[272,512]{1,0:T(8,128)(2,1)S(1)}, u32[]{:S(2)}, u32[]{:S(2)}) collective-permute-start(bf16[272,512]{1,0:T(8,128)(2,1)S(1)} %add_select_fusion), channel_id=1, source_target_pairs={{0,4},{2,6},{4,0},{6,2},{8,12},{10,14},{12,8},{14,10},{16,20},{18,... | collective-permute-start | bytes 835592 | tf_op jit(solution)/shard_map/ppermute | solution.py:276
  40.5 7.2 %collective-permute-start.9 = (bf16[272,512]{1,0:T(8,128)(2,1)S(1)}, bf16[272,512]{1,0:T(8,128)(2,1)S(1)}, u32[]{:S(2)}, u32[]{:S(2)}) collective-permute-start(bf16[272,512]{1,0:T(8,128)(2,1)S(1)} %add_select_fusion), channel_id=1, source_target_pairs={{0,6},{2,0},{4,2},{6,4},{8,14},{10,8},{12,10},{14,12},{16,22},{18,... | collective-permute-start | bytes 835592 | tf_op jit(solution)/shard_map/ppermute | solution.py:276
  47.7 2.4 %copy-start.5 = (f32[768]{0:T(1024)S(1)}, f32[768]{0:T(1024)}, u32[]{:S(2)}) copy-start(f32[768]{0:T(1024)} %get-tuple-element.22) | copy-start | bytes 9220
  47.9 16.4 %collective-permute-start.10 = (bf16[4,272,512]{2,1,0:T(8,128)(2,1)S(1)}, bf16[4,272,512]{2,1,0:T(8,128)(2,1)S(1)}, u32[]{:S(2)}, u32[]{:S(2)}) collective-permute-start(bf16[4,272,512]{2,1,0:T(8,128)(2,1)S(1)} %get-tuple-element.16), channel_id=1, source_target_pairs={{0,1},{1,0},{2,3},{3,2},{4,5},{5,4},{6,7},{7,6},{8,9},{9,8},{10,11... | collective-permute-start | bytes 3342344 | tf_op jit(solution)/shard_map/ppermute | solution.py:276
  105.2 25.9 %all-to-all-start.1 = ((f32[32,16,512]{2,1,0:T(8,128)}), f32[32,16,512]{2,1,0:T(8,128)S(1)}, u32[]{:S(2)}, u32[]{:S(2)}) async-start(f32[32,16,512]{2,1,0:T(8,128)} %broadcast_in_dim.15), calls=%async_computation.1 | async-start | bytes 2097152 | tf_op jit(solution)/shard_map/all_to_all | solution.py:339
  114.1 74.4 %all-reduce.2.cloned.1.call-start = ((), (), s32[]{:S(2)}) async-start(), calls=%async_computation.2 | async-start | bytes 3145728 | tf_op jit(solution)/shard_map/psum | solution.py:337
  131.1 1.0 copy-start.1
Sparse Core Ops, SparseCore 0:
  117.2 71.2 all-reduce.1

commit v2 on v1

v2 whole, which is shorter than its diff:
```python
import functools
import math

import jax
import jax.numpy as jnp
import numpy as np
from jax import lax
from jax.experimental import pallas as pl
from jax.experimental.pallas import tpu as pltpu
from jax.sharding import PartitionSpec as P


PANEL = 512
SIDE = 4
SAMPLE_BLOCK = 512
EXTRA = 16
HIGHEST = lax.Precision.HIGHEST
NT = (((1,), (1,)), ((), ()))
TN = (((0,), (0,)), ((), ()))
INV_TURN = 1.0 / (2.0 * math.pi)
DEGREE = 4
MAGIC = 12582912.0


def sine_coefficients():
    u = np.cos(np.pi * (np.arange(4000) + 0.5) / 4000) * 0.25
    fit = np.polynomial.chebyshev.Chebyshev.fit(u * u, -np.sin(2 * np.pi * u) / u, DEGREE, domain=[0, 1 / 16])
    poly = fit.convert(kind=np.polynomial.Polynomial, domain=[-1, 1], window=[-1, 1])
    return [float(v) for v in poly.coef]


SINE = sine_coefficients()


def scaled_cos(turns, scale):
    r = turns - ((turns + MAGIC) - MAGIC)
    u = jnp.abs(r) - 0.25
    s = u * u
    coefs = [v * scale for v in SINE]
    p = coefs[DEGREE]
    for v in coefs[DEGREE - 1::-1]:
        p = p * s + v
    return p * u


def column(line):
    n = line.shape[1]
    eye = lax.broadcasted_iota(jnp.int32, (128, 128), 0) == lax.broadcasted_iota(jnp.int32, (128, 128), 1)
    parts = []
    for q in range(n // 128):
        square = jnp.broadcast_to(line[:, 128 * q:128 * q + 128], (128, 128))
        parts.append(jnp.sum(jnp.where(eye, square, 0.0), axis=1, keepdims=True))
    return jnp.concatenate(parts, axis=0)


def local_kernel(w_ref, ph_ref, x_ref, *refs, scale):
    o_ref, col_ref = refs[-2:]

    @pl.when(pl.program_id(0) == 0)
    def _():
        col_ref[...] = column(ph_ref[...])

    proj = lax.dot_general(w_ref[...], x_ref[...], NT, preferred_element_type=jnp.float32)
    o_ref[...] = scaled_cos(proj * INV_TURN + col_ref[...], scale).astype(jnp.bfloat16)


def local_features(wt, turns, data, scale, first, blocks, bs, before=None):
    rows, din = wt.shape
    samples = data.shape[0]
    done = [] if before is None else [before]
    return pl.pallas_call(
        functools.partial(local_kernel, scale=scale),
        grid=(blocks,),
        in_specs=[
            pl.BlockSpec((rows, din), lambda i: (0, 0)),
            pl.BlockSpec((1, rows), lambda i: (0, 0)),
            pl.BlockSpec((bs, din), lambda i: (first + i, 0)),
            *[pl.BlockSpec(memory_space=pl.ANY) for _ in done],
        ],
        out_specs=pl.BlockSpec((rows, bs), lambda i: (0, first + i)),
        out_shape=jax.ShapeDtypeStruct((rows, samples), jnp.bfloat16),
        scratch_shapes=[pltpu.VMEM((rows, 1), jnp.float32)],
        input_output_aliases={3: 0} if done else {},
        cost_estimate=pl.CostEstimate(flops=2 * rows * blocks * bs * din, bytes_accessed=3 * blocks * bs * din, transcendentals=0),
        name="local_features",
    )(wt, turns, data, *done)


def place_of(feat):
    return lax.div(feat, 2 * SIDE), lax.rem(lax.div(feat, 2), SIDE), lax.rem(feat, 2)


def gram_kernel(feat_ref, *refs, scale, sub):
    slots, (x_ref, f_ref, e_ref, s_ref, d_ref, v_ref, acc_ref, ph_ref, panel_ref) = refs[:8], refs[8:]
    i = pl.program_id(0)
    rows = s_ref.shape[0]
    y, x, c = place_of(feat_ref[0])
    first = pl.multiple_of(feat_ref[0] * 16, 16)

    def sixteen(p):
        within = pl.ds(pl.multiple_of(lax.rem(first, 256), 16), 16)
        return v_ref[p + lax.div(first, 256), within, :]

    def add(cols, left, right, sign):
        out = lax.dot_general(left, right, NT, preferred_element_type=jnp.float32)
        s_ref[:, cols] += sign * out[:rows]
        acc_ref[:, cols] += sign * out[rows:]

    @pl.when(i == 0)
    def _():
        for k in range(SIDE):
            along_x = lax.rem(x - k + SIDE, SIDE)
            along_y = SIDE + lax.rem(y - k + SIDE, SIDE)
            v_ref[jnp.where(c == 0, along_x, along_y)] = slots[k][...]
            v_ref[jnp.where(c == 0, along_y, along_x)] = slots[SIDE + k][...]
        tail = v_ref[0, 256:256 + EXTRA, :].astype(jnp.float32)
        ph_ref[...] = column((tail[0:1] + tail[1:2]) + tail[2:3])
        s_ref[...] = jnp.zeros_like(s_ref)
        acc_ref[...] = jnp.zeros_like(acc_ref)

    for chunk in range(3):
        @pl.when(i == chunk)
        def _(chunk=chunk):
            left = jnp.concatenate([e_ref[...], sixteen(2 + 2 * chunk)], axis=0)
            for h in range(2):
                add(slice(256 * h, 256 * h + 256), left, v_ref[2 + 2 * chunk + h, :256, :], -1.0)

    for j in range(x_ref.shape[0] // sub):
        at = slice(j * sub, j * sub + sub)
        for h in range(2):
            half = slice(256 * h, 256 * h + 256)
            proj = lax.dot_general(v_ref[h, :256, :], x_ref[at, :], NT, preferred_element_type=jnp.float32)
            panel_ref[j, half, :] = scaled_cos(proj * INV_TURN + ph_ref[half, :], scale).astype(jnp.bfloat16)
        mine = panel_ref[j, pl.ds(first, 16), :]
        left = jnp.concatenate([f_ref[:, at], mine], axis=0)
        for h in range(2):
            half = slice(256 * h, 256 * h + 256)
            add(half, left, panel_ref[j, half, :], 1.0)

    @pl.when(i == pl.num_programs(0) - 1)
    def _():
        for k in range(d_ref.shape[0]):
            d_ref[k] = acc_ref[...]


def gram(feat, slots, data, local, earlier, scale, copies, bs=1024, sub=512):
    rows = earlier.shape[0]
    samples, din = data.shape
    return pl.pallas_call(
        functools.partial(gram_kernel, scale=scale, sub=sub),
        grid=(samples // bs,),
        in_specs=[
            pl.BlockSpec(memory_space=pltpu.SMEM),
            *[pl.BlockSpec(v.shape, lambda i: (0, 0)) for v in slots],
            pl.BlockSpec((bs, din), lambda i: (i, 0)),
            pl.BlockSpec((rows, bs), lambda i: (0, i)),
            pl.BlockSpec((rows, PANEL), lambda i: (0, jnp.minimum(i, 2))),
        ],
        out_specs=[
            pl.BlockSpec((rows, PANEL), lambda i: (0, 0)),
            pl.BlockSpec((copies, 16, PANEL), lambda i: (0, 0, 0)),
        ],
        out_shape=[
            jax.ShapeDtypeStruct((rows, PANEL), jnp.float32),
            jax.ShapeDtypeStruct((copies, 16, PANEL), jnp.float32),
        ],
        scratch_shapes=[
            pltpu.VMEM((2 * SIDE, *slots[0].shape), jnp.bfloat16),
            pltpu.VMEM((16, PANEL), jnp.float32),
            pltpu.VMEM((PANEL, 1), jnp.float32),
            pltpu.VMEM((bs // sub, PANEL, sub), jnp.bfloat16),
        ],
        cost_estimate=pl.CostEstimate(flops=8 << 30, bytes_accessed=16 << 20, transcendentals=0),
        name="gram",
    )(feat, *slots, data, local, earlier)


def split2(v):
    high = v.astype(jnp.bfloat16)
    return high, (v - high.astype(jnp.float32)).astype(jnp.bfloat16)


def split3(v):
    high = v.astype(jnp.bfloat16)
    rest = v - high.astype(jnp.float32)
    mid = rest.astype(jnp.bfloat16)
    return high, mid, (rest - mid.astype(jnp.float32)).astype(jnp.bfloat16)


def spread(block, j):
    return jnp.broadcast_to(block[:, j:j + 1], (8, 128))


def block_inverse(n_ref, lb_ref):
    sub = lax.broadcasted_iota(jnp.int32, (8, 128), 0)
    lane = lax.broadcasted_iota(jnp.int32, (8, 128), 1)

    def step(s, carry):
        rows0, rows1, left, right = carry
        k = pl.multiple_of(s * 8, 8)
        shift = jnp.where(s == 0, 0, 128 - k)
        n_ref[...] -= lax.dot_general(left, right, TN, preferred_element_type=jnp.float32)
        pivot = pltpu.roll(rows0, shift, 1)
        a = [[None] * 8 for _ in range(8)]
        for j in range(8):
            col = spread(pivot, j)
            for i in range(j, 8):
                a[i][j] = jnp.broadcast_to(col[i:i + 1, :], (8, 128))
        low = [[None] * 8 for _ in range(8)]
        root = []
        for j in range(8):
            inverse = 1.0 / a[j][j]
            root.append(lax.rsqrt(a[j][j]))
            for i in range(j + 1, 8):
                low[i][j] = a[i][j] * inverse
            for i in range(j + 1, 8):
                for m in range(j + 1, i + 1):
                    a[i][m] = a[i][m] - low[i][j] * a[m][j]
        t = [[None] * 8 for _ in range(8)]
        for j in range(8):
            t[j][j] = root[j]
            for i in range(j + 1, 8):
                acc = low[i][j]
                for m in range(j + 1, i):
                    acc = acc + low[i][m] * t[m][j]
                t[i][j] = -acc
        for j in range(8):
            for i in range(j + 1, 8):
                t[i][j] = root[i] * t[i][j]
        w0 = jnp.zeros((8, 128), jnp.float32)
        w1 = jnp.zeros((8, 128), jnp.float32)
        for j in range(8):
            col = jnp.where(sub == j, t[j][j], 0.0)
            for i in range(j + 1, 8):
                col = jnp.where(sub == i, t[i][j], col)
            w0 = w0 + col * jnp.broadcast_to(rows0[j:j + 1, :], (8, 128))
            w1 = w1 + col * jnp.broadcast_to(rows1[j:j + 1, :], (8, 128))
        lb_ref[pl.ds(k, 8), :] = w1
        after = jnp.minimum(k + 8, 120)
        after = pl.multiple_of(after, 8)
        next0 = n_ref[pl.ds(after, 8), :128]
        next1 = n_ref[pl.ds(after, 8), 128:]
        cross = pltpu.roll(next0, shift, 1)
        cols = [spread(cross, m) for m in range(8)]
        for j in range(8):
            factor = t[j][0] * cols[0]
            for m in range(1, j + 1):
                factor = factor + t[j][m] * cols[m]
            next0 = next0 - factor * jnp.broadcast_to(w0[j:j + 1, :], (8, 128))
            next1 = next1 - factor * jnp.broadcast_to(w1[j:j + 1, :], (8, 128))
        gh, gm, gl = split3(jnp.where(lane >= k + 8, w0, 0.0))
        wh, wm, wl = split3(jnp.concatenate([w0, w1], axis=1))
        left = jnp.concatenate([gh, gh, gm, gh, gm, gl], axis=0)
        right = jnp.concatenate([wh, wm, wh, wl, wm, wh], axis=0)
        return next0, next1, left, right

    start = (
        n_ref[:8, :128],
        n_ref[:8, 128:],
        jnp.zeros((48, 128), jnp.bfloat16),
        jnp.zeros((48, 256), jnp.bfloat16),
    )
    lax.fori_loop(0, 16, step, start)


def factor_kernel(ridge_ref, d_ref, out_ref, m_ref, j_ref, n_ref, lb_ref):
    n = PANEL
    eye = lax.broadcasted_iota(jnp.int32, (n, n), 0) == lax.broadcasted_iota(jnp.int32, (n, n), 1)
    m_ref[...] = d_ref[...].reshape(n, n) + jnp.where(eye, ridge_ref[0], 0.0)
    j_ref[...] = jnp.where(eye, 1.0, 0.0)
    out_ref[...] = jnp.zeros((n, n), jnp.float32)
    small = lax.broadcasted_iota(jnp.int32, (128, 128), 0) == lax.broadcasted_iota(jnp.int32, (128, 128), 1)
    for b in range(n // 128):
        r0, r1 = 128 * b, 128 * b + 128
        n_ref[:, :128] = m_ref[r0:r1, r0:r1]
        n_ref[:, 128:] = jnp.where(small, 1.0, 0.0)
        block_inverse(n_ref, lb_ref)
        lb = lb_ref[...]
        jb = jnp.dot(lb, j_ref[r0:r1, :r1], precision=HIGHEST, preferred_element_type=jnp.float32)
        out_ref[r0:r1, :r1] = jb
        if r1 < n:
            r = jnp.dot(lb, m_ref[r0:r1, r1:], precision=HIGHEST, preferred_element_type=jnp.float32)
            m_ref[r1:, r1:] -= lax.dot_general(r, r, TN, precision=HIGHEST, preferred_element_type=jnp.float32)
            j_ref[r1:, :r1] -= lax.dot_general(r, jb, TN, precision=HIGHEST, preferred_element_type=jnp.float32)


def factor_inverse(ridge, d):
    n = PANEL
    return pl.pallas_call(
        factor_kernel,
        out_shape=jax.ShapeDtypeStruct((n, n), jnp.float32),
        in_specs=[pl.BlockSpec(memory_space=pltpu.SMEM), pl.BlockSpec(memory_space=pltpu.VMEM)],
        out_specs=pl.BlockSpec(memory_space=pltpu.VMEM),
        scratch_shapes=[
            pltpu.VMEM((n, n), jnp.float32),
            pltpu.VMEM((n, n), jnp.float32),
            pltpu.VMEM((128, 256), jnp.float32),
            pltpu.VMEM((128, 128), jnp.float32),
        ],
        cost_estimate=pl.CostEstimate(flops=8 << 30, bytes_accessed=2 << 20, transcendentals=0),
        name="factor_inverse",
    )(ridge, d)


def solve_kernel(feat_ref, ridge_ref, s_ref, inv_ref, o_ref, *, rows):
    bs = s_ref.shape[0]
    row_ids = feat_ref[0] * rows + pl.program_id(0) * bs + lax.broadcasted_iota(jnp.int32, (bs, PANEL), 0)
    hit = row_ids == lax.broadcasted_iota(jnp.int32, (bs, PANEL), 1)
    sh, sl = split2(s_ref[...] + jnp.where(hit, ridge_ref[0], 0.0))
    for b in range(PANEL // 256):
        r0, r1 = 256 * b, 256 * b + 256
        lh, ll = split2(inv_ref[r0:r1, :r1])
        out = lax.dot_general(sh[:, :r1], ll, NT, preferred_element_type=jnp.float32)
        out += lax.dot_general(sl[:, :r1], lh, NT, preferred_element_type=jnp.float32)
        o_ref[:, r0:r1] = out + lax.dot_general(sh[:, :r1], lh, NT, preferred_element_type=jnp.float32)


def solve(feat, ridge, s, inverse, bs=256):
    rows = s.shape[0]
    smem = pl.BlockSpec(memory_space=pltpu.SMEM)
    return pl.pallas_call(
        functools.partial(solve_kernel, rows=rows),
        grid=(rows // bs,),
        out_shape=jax.ShapeDtypeStruct(s.shape, jnp.float32),
        in_specs=[smem, smem, pl.BlockSpec((bs, PANEL), lambda i: (i, 0)), pl.BlockSpec((PANEL, PANEL), lambda i: (0, 0))],
        out_specs=pl.BlockSpec((bs, PANEL), lambda i: (i, 0)),
        cost_estimate=pl.CostEstimate(flops=6 * rows * PANEL * PANEL, bytes_accessed=4 << 20, transcendentals=0),
        name="solve",
    )(feat, ridge, s, inverse)


def feat_of(y, x, c):
    return ((y % SIDE) * SIDE + x % SIDE) * 2 + c


def permute(value, pairs):
    return lax.ppermute(value, "feat", pairs)


def share_panel(weights, earlier, tail, y, x, c):
    side = range(SIDE)
    root = (feat_of(0, 0, 0), feat_of(0, 0, 1))
    other = permute(earlier[:PANEL, PANEL:3 * PANEL], [root])

    def first_half(k):
        return weights[256 * k:256 * k + 256] if k < 2 else earlier[256 * (k - 2):256 * (k - 1), :PANEL]

    def last_half(k):
        return other[256 * (k % 2):256 * (k % 2) + 256, PANEL * (k // 2):PANEL * (k // 2) + PANEL]

    half = [jnp.where(c == 0, first_half(k), last_half(k)) for k in side]
    got = [permute(half[k], [(root[0], feat_of(0, k, 0)), (root[1], feat_of(k, 0, 1))]) for k in (2, 1, 3)]
    held = jnp.where((x == 0) & (y == 0), half[0], got[0] + got[1] + got[2])
    held = jnp.concatenate([held, tail])
    got = [
        permute(
            held,
            [(feat_of(0, j, 0), feat_of(k, j, 0)) for j in side] + [(feat_of(j, 0, 1), feat_of(j, k, 1)) for j in side],
        )
        for k in (2, 1, 3)
    ]
    held = jnp.where(jnp.where(c == 0, y, x) == 0, held, got[0] + got[1] + got[2])
    own = [held] + [
        permute(
            held,
            [(feat_of(i, j, 0), feat_of(i, j + k, 0)) for i in side for j in side]
            + [(feat_of(i, j, 1), feat_of(i + k, j, 1)) for i in side for j in side],
        )
        for k in (1, 2, 3)
    ]
    partner = [permute(own[k], [(i, i ^ 1) for i in range(2 * SIDE * SIDE)]) for k in side]
    return own + partner


def on_device(data, omega, phase, earlier, ridge):
    samp, planes = lax.axis_size("samp"), lax.axis_size("feat")
    scale = math.sqrt(2.0 / (data.shape[0] * samp))
    feat = lax.axis_index("feat")
    y, x, c = place_of(feat)
    feat = feat.reshape(1)

    weights = omega.T
    turns = phase * INV_TURN
    high = lax.reduce_precision(turns, 8, 7)
    mid = lax.reduce_precision(turns - high, 8, 7)
    low = turns - high - mid
    tail = jnp.stack([high[:PANEL], mid[:PANEL], low[:PANEL]]).astype(jnp.bfloat16)
    tail = jnp.concatenate([tail, jnp.zeros((EXTRA - 3, PANEL), jnp.bfloat16)])
    slots = share_panel(weights, earlier, tail, y, x, c)

    local = None
    blocks = data.shape[0] // SAMPLE_BLOCK
    for part, first in enumerate((0, blocks // 4, blocks // 2)):
        count = blocks // 2 if part == 2 else blocks // 4
        local = local_features(weights, turns[None], data, scale, first, count, SAMPLE_BLOCK, local)
    s, d = gram(feat, slots, data, local, earlier, scale, samp)
    summed = lax.psum(s, "samp")
    d = lax.all_to_all(d, "samp", 0, 0).sum(0)
    d = lax.all_to_all(jnp.broadcast_to(d, (planes, 16, PANEL)), "feat", 0, 0)
    inverse = factor_inverse(ridge, d)
    return solve(feat, ridge, summed, inverse)


def solution(mesh):
    in_specs = (P("samp", None), P(None, "feat"), P("feat"), P("feat", "samp"), P())
    out_specs = P("feat", None)
    return jax.shard_map(on_device, mesh=mesh, in_specs=in_specs, out_specs=out_specs, check_vma=False)
```

time: 203 us -> 200 us (0.985)
  other arithmetic: 4.78 us -> 1.26 us
  local copies, waits for them, and re-layouts: 10.2 us -> 6.74 us
  starting transfers between devices: 27 us -> 29.1 us
    pallas_call x1, Pallas kernels: 34.8 us -> 29.4 us  [factor_inverse(): pl.pallas_call(factor_kernel, out_shape=jax.ShapeDtypeStruct((n, n), jnp....]
    psum x1, waiting for transfers between devices: 21.6 us -> 26.6 us  [on_device(): summed = lax.psum(s, 'samp')]
    pallas_call x3 -> x5, Pallas kernels: 35.1 us -> 39.3 us  [the longest x3 18.3 us: local_features(): pl.pallas_call(functools.partial(local_kernel, scale=scale), grid=(blocks...]
    ppermute x11 -> x14, starting transfers between devices: 18.1 us -> 22.1 us  [permute(): return lax.ppermute(value, 'feat', pairs)]
    ppermute x11 -> x14, waiting for transfers between devices: 16.2 us -> 12.4 us  [permute(): return lax.ppermute(value, 'feat', pairs)]
    concatenate x8 -> x1, local copies, waits for them, and re-layouts: 2.72 us -> 0.26 us  [share_panel(): held = jnp.concatenate([held, tail])]
    all_to_all x1, starting transfers between devices: 8.83 us -> 6.75 us  [on_device(): d = lax.all_to_all(jnp.broadcast_to(d, (planes, 16, PANEL)), 'feat', 0, 0)]
  transfers between devices with their start and end apart: 13 -> 16, of which waited for: 9 -> 8; matrix products, arithmetic and copies ran while one was open for 2% -> 1% of each run, Pallas kernels for 24% -> 24%
where the time goes in v2:
time: 200 us; the launch traced here: 196 us
  Pallas kernels  68.8 us (34%)
  waiting for transfers between devices  55.1 us (28%)
  starting transfers between devices  29.1 us (15%)
  blocking collectives  20.4 us (10%)
  between operations  14.3 us (7%)
  local copies, waits for them, and re-layouts  6.74 us (3%)
    pallas_call x1, Pallas kernels, factor_inverse(): pl.pallas_call(factor_kernel, out_shape=jax.ShapeDtypeStruct((n, n), jnp....  29.4 us
    psum x1, waiting for transfers between devices, on_device(): summed = lax.psum(s, 'samp')  26.6 us
    ppermute x14, starting transfers between devices, permute(): return lax.ppermute(value, 'feat', pairs)  22.1 us
    all_to_all x1, blocking collectives, on_device(): d = lax.all_to_all(d, 'samp', 0, 0).sum(0)  20.4 us
    pallas_call x3, Pallas kernels, local_features(): pl.pallas_call(functools.partial(local_kernel, scale=scale), grid=(blocks...  18.3 us
    pallas_call x1, Pallas kernels, gram(): pl.pallas_call(functools.partial(gram_kernel, scale=scale, sub=sub), grid...  16.4 us
    all_to_all x1, waiting for transfers between devices, on_device(): d = lax.all_to_all(jnp.broadcast_to(d, (planes, 16, PANEL)), 'feat', 0, 0)  15.7 us
    ppermute x14, waiting for transfers between devices, permute(): return lax.ppermute(value, 'feat', pairs)  12.4 us
  transfers between devices with their start and end apart: 16, of which 8 were waited for; matrix products, arithmetic and copies ran while one was open for 1% of the time, Pallas kernels for 24%

profile of v2, /device:TPU:1, one launch (start us, length us, event | category | flops | bytes accessed | tf_op | source)
XLA Modules:
  0.0 195.7 jit_solution(10783645819871766120)
XLA Ops:
  6.5 1.3 slice.40
  7.8 0.0 copy-start.3
  7.8 1.3 collective-permute-start
  9.2 1.4 copy.8
  10.6 0.0 copy-start
  10.6 3.9 %collective-permute-done = bf16[512,1024]{1,0:T(8,128)(2,1)S(1)} collective-permute-done((bf16[512,1024]{1,0:T(8,128)(2,1)S(1)}, bf16[512,1024]{1,0:T(8,128)(2,1)S(1)}, u32[]{:S(2)}, u32[]{:S(2)}) %collective-permute-start) | collective-permute-done | bytes 1048608 | tf_op jit(solution)/shard_map/ppermute | solution.py:337
  14.5 1.1 slice_select_fusion.2
  15.6 1.5 collective-permute-start.1
  17.1 1.3 collective-permute-start.2
  18.4 1.3 collective-permute-start.3
  19.8 0.5 collective-permute-done.1
  20.4 2.8 %collective-permute-done.2 = bf16[256,512]{1,0:T(8,128)(2,1)S(1)} collective-permute-done((bf16[256,512]{1,0:T(8,128)(2,1)S(1)}, bf16[256,512]{1,0:T(8,128)(2,1)S(1)}, u32[]{:S(2)}, u32[]{:S(2)}) %collective-permute-start.2) | collective-permute-done | bytes 262176 | tf_op jit(solution)/shard_map/ppermute | solution.py:337
  23.2 0.1 fusion
  23.3 0.3 concatenate.4
  23.5 1.3 collective-permute-start.4
  24.8 1.3 collective-permute-start.5
  26.1 1.3 collective-permute-start.6
  27.5 0.8 collective-permute-done.4
  28.3 3.0 %collective-permute-done.5 = bf16[272,512]{1,0:T(8,128)(2,1)S(1)} collective-permute-done((bf16[272,512]{1,0:T(8,128)(2,1)S(1)}, bf16[272,512]{1,0:T(8,128)(2,1)S(1)}, u32[]{:S(2)}, u32[]{:S(2)}) %collective-permute-start.5) | collective-permute-done | bytes 278560 | tf_op jit(solution)/shard_map/ppermute | solution.py:337
  31.3 0.1 add_select_fusion.refs_0_
  31.4 2.0 %collective-permute-start.7 = (bf16[272,512]{1,0:T(8,128)(2,1)S(1)}, bf16[272,512]{1,0:T(8,128)(2,1)S(1)}, u32[]{:S(2)}, u32[]{:S(2)}) collective-permute-start(bf16[272,512]{1,0:T(8,128)(2,1)S(1)} %add_select_fusion.refs_0_), channel_id=1, source_target_pairs={{0,2},{2,4},{4,6},{6,0},{8,10},{10,12},{12,14},{14,8},{16,18},{18,... | collective-permute-start | bytes 835592 | tf_op jit(solution)/shard_map/ppermute | solution.py:337
  33.3 2.2 %collective-permute-start.8 = (bf16[272,512]{1,0:T(8,128)(2,1)S(1)}, bf16[272,512]{1,0:T(8,128)(2,1)S(1)}, u32[]{:S(2)}, u32[]{:S(2)}) collective-permute-start(bf16[272,512]{1,0:T(8,128)(2,1)S(1)} %add_select_fusion.refs_0_), channel_id=1, source_target_pairs={{0,4},{2,6},{4,0},{6,2},{8,12},{10,14},{12,8},{14,10},{16,20},{18,... | collective-permute-start | bytes 835592 | tf_op jit(solution)/shard_map/ppermute | solution.py:337
  35.5 0.3 collective-permute-start.9
  35.8 0.6 broadcast_in_dim.12.ph_ref
  36.4 2.8 %collective-permute-start.10 = (bf16[272,512]{1,0:T(8,128)(2,1)S(1)}, bf16[272,512]{1,0:T(8,128)(2,1)S(1)}, u32[]{:S(2)}, u32[]{:S(2)}) collective-permute-start(bf16[272,512]{1,0:T(8,128)(2,1)S(1)} %add_select_fusion.refs_0_), channel_id=1, source_target_pairs={{0,1},{1,0},{2,3},{3,2},{4,5},{5,4},{6,7},{7,6},{8,9},{9,8},{10,11... | collective-permute-start | bytes 835592 | tf_op jit(solution)/shard_map/ppermute | solution.py:337
  39.2 2.2 %collective-permute-start.11 = (bf16[272,512]{1,0:T(8,128)(2,1)S(1)}, bf16[272,512]{1,0:T(8,128)(2,1)S(1)}, u32[]{:S(2)}, u32[]{:S(2)}) collective-permute-start(bf16[272,512]{1,0:T(8,128)(2,1)S(1)} %collective-permute-done.7.refs_1_), channel_id=1, source_target_pairs={{0,1},{1,0},{2,3},{3,2},{4,5},{5,4},{6,7},{7,6},{8,9},{9,8},{10,11... | collective-permute-start | bytes 835592 | tf_op jit(solution)/shard_map/ppermute | solution.py:337
  41.4 1.4 collective-permute-done.8.refs_2_
  42.8 3.1 %collective-permute-start.12 = (bf16[272,512]{1,0:T(8,128)(2,1)S(1)}, bf16[272,512]{1,0:T(8,128)(2,1)S(1)}, u32[]{:S(2)}, u32[]{:S(2)}) collective-permute-start(bf16[272,512]{1,0:T(8,128)(2,1)S(1)} %collective-permute-done.8.refs_2_), channel_id=1, source_target_pairs={{0,1},{1,0},{2,3},{3,2},{4,5},{5,4},{6,7},{7,6},{8,9},{9,8},{10,11... | collective-permute-start | bytes 835592 | tf_op jit(solution)/shard_map/ppermute | solution.py:337
  45.9 0.3 collective-permute-start.13
  46.1 5.2 %local_features.3.refs_0_ = bf16[768,4096]{1,0:T(8,128)(2,1)} custom-call(bf16[768,512]{1,0:T(8,128)(2,1)} %bitcast.4, f32[1,768]{1,0:T(1,128)} %broadcast_in_dim.12.ph_ref, bf16[4096,512]{1,0:T(8,128)(2,1)} %refs_8_.1), custom_call_target="tpu_custom_call" | custom-call | flops 805306368 | bytes 1572864 | tf_op jit(solution)/shard_map/local_features/pallas_call | solution.py:71
  51.3 5.3 %local_features.4.refs_0_ = bf16[768,4096]{1,0:T(8,128)(2,1)} custom-call(bf16[768,512]{1,0:T(8,128)(2,1)} %bitcast.5, f32[1,768]{1,0:T(1,128)} %broadcast_in_dim.12.ph_ref, bf16[4096,512]{1,0:T(8,128)(2,1)} %refs_8_.1, bf16[768,4096]{1,0:T(8,128)(2,1)} %local_features.3.refs_0_), custom_call_target="tpu_custom_call", output_to_operand_aliasing={{}: (3, {})} | custom-call | flops 805306368 | bytes 1572864 | tf_op jit(solution)/shard_map/local_features/pallas_call | solution.py:71
  56.6 7.9 %local_features.5.refs_9_ = bf16[768,4096]{1,0:T(8,128)(2,1)} custom-call(bf16[768,512]{1,0:T(8,128)(2,1)} %bitcast.6, f32[1,768]{1,0:T(1,128)} %broadcast_in_dim.12.ph_ref, bf16[4096,512]{1,0:T(8,128)(2,1)} %refs_8_.1, bf16[768,4096]{1,0:T(8,128)(2,1)} %local_features.4.refs_0_), custom_call_target="tpu_custom_call", output_to_operand_aliasing={{}: (3, {})} | custom-call | flops 1610612736 | bytes 3145728 | tf_op jit(solution)/shard_map/local_features/pallas_call | solution.py:71
  64.5 0.0 collective-permute-done.11.refs_5_
  64.6 0.7 copy-done.7
  65.2 0.1 copy-done.8
  65.3 0.1 copy-done.9
  65.5 0.1 copy-done.10
  65.6 16.4 %gram.1 = (f32[768,512]{1,0:T(8,128)}, f32[8,16,512]{2,1,0:T(8,128)}) custom-call(s32[1]{0:T(128)} %bitcast.feat_ref, bf16[272,512]{1,0:T(8,128)(2,1)} %copy-done.2, bf16[272,512]{1,0:T(8,128)(2,1)} %copy-done.4, bf16[272,512]{1,0:T(8,128)(2,1)} %copy-done.5, bf16[272,512]{1,0:T(8,128)(2,1)} %copy-done.6, bf16[272,512]{1,0:T(8,128)(2,1)} %copy-done.7, ...), custom_call_target="tpu_custom_call" | custom-call | flops 8589934592 | bytes 16777216 | tf_op jit(solution)/shard_map/gram/pallas_call | solution.py:149
  82.0 20.4 %all_to_all.10 = f32[8,16,512]{2,1,0:T(8,128)S(1)} all-to-all(f32[8,16,512]{2,1,0:T(8,128)} %get-tuple-element.8), channel_id=1, replica_groups=mesh['samp'=8,'feat'=32] {'samp'}, dimensions={0} | all-to-all | bytes 524288 | tf_op jit(solution)/shard_map/all_to_all | solution.py:398
  102.4 1.1 broadcast_in_dim.13
  103.5 6.7 %all-to-all-start.1 = ((f32[32,16,512]{2,1,0:T(8,128)}), f32[32,16,512]{2,1,0:T(8,128)S(1)}, u32[]{:S(2)}, u32[]{:S(2)}) async-start(f32[32,16,512]{2,1,0:T(8,128)} %broadcast_in_dim.13), calls=%async_computation.1 | async-start | bytes 2097152 | tf_op jit(solution)/shard_map/all_to_all | solution.py:399
  110.2 0.3 all-reduce.2.cloned.1.call-start
  110.5 0.5 all-reduce.2.cloned.1.call-update
  111.6 15.7 %all-to-all-done.1.d_ref = f32[32,16,512]{2,1,0:T(8,128)S(1)} async-done(((f32[32,16,512]{2,1,0:T(8,128)}), f32[32,16,512]{2,1,0:T(8,128)S(1)}, u32[]{:S(2)}, u32[]{:S(2)}) %all-to-all-start.1) | async-done | bytes 1048608 | tf_op jit(solution)/shard_map/all_to_all | solution.py:399
  127.3 1.0 copy-done.1
  128.3 29.4 %factor_inverse.1.inv_ref = f32[512,512]{1,0:T(8,128)} custom-call(f32[1]{0:T(128)S(6)} %copy.12.ridge_ref, f32[32,16,512]{2,1,0:T(8,128)} %copy-done.1), custom_call_target="tpu_custom_call" | custom-call | flops 8589934592 | bytes 2097152 | tf_op jit(solution)/shard_map/factor_inverse/pallas_call | solution.py:289
  157.7 26.6 %all-reduce.2.cloned.1.call-done.s_ref = f32[768,512]{1,0:T(8,128)} async-done(((f32[768,512]{1,0:T(8,128)}), f32[768,512]{1,0:T(8,128)}) %all-reduce.2.cloned.1.call-update) | async-done | bytes 1572880 | tf_op jit(solution)/shard_map/psum | solution.py:397
  184.3 4.6 %solve.1 = f32[768,512]{1,0:T(8,128)} custom-call(s32[1]{0:T(128)} %bitcast.feat_ref, f32[1]{0:T(128)S(6)} %copy.12.ridge_ref, f32[768,512]{1,0:T(8,128)} %all-reduce.2.cloned.1.call-done.s_ref, f32[512,512]{1,0:T(8,128)} %factor_inverse.1.inv_ref), custom_call_target="tpu_custom_call" | custom-call | flops 1207959552 | bytes 4194304 | tf_op jit(solution)/shard_map/solve/pallas_call | solution.py:321
  (31 shorter events, 0.1 us)
Async XLA Ops:
  7.8 11.9 %copy-start.3 = (f32[768]{0:T(1024)S(1)}, f32[768]{0:T(1024)}, u32[]{:S(2)}) copy-start(f32[768]{0:T(1024)} %param.7) | copy-start | bytes 9220
  7.8 6.6 %collective-permute-start = (bf16[512,1024]{1,0:T(8,128)(2,1)S(1)}, bf16[512,1024]{1,0:T(8,128)(2,1)S(1)}, u32[]{:S(2)}, u32[]{:S(2)}) collective-permute-start(bf16[512,1024]{1,0:T(8,128)(2,1)S(1)} %slice.40), channel_id=1, source_target_pairs={{0,1},{32,33},{64,65},{96,97},{128,129},{160,161},{192,193},{224,2... | collective-permute-start | bytes 3145736 | tf_op jit(solution)/shard_map/ppermute | solution.py:337
  10.6 20.8 %copy-start = (bf16[512,768]{0,1:T(8,128)(2,1)}, bf16[512,768]{0,1:T(8,128)(2,1)S(1)}, u32[]{:S(2)}) copy-start(bf16[512,768]{0,1:T(8,128)(2,1)S(1)} %copy.8) | copy-start | bytes 2359300
  15.6 4.8 %collective-permute-start.1 = (bf16[256,512]{1,0:T(8,128)(2,1)S(1)}, bf16[256,512]{1,0:T(8,128)(2,1)S(1)}, u32[]{:S(2)}, u32[]{:S(2)}) collective-permute-start(bf16[256,512]{1,0:T(8,128)(2,1)S(1)} %get-tuple-element.9), channel_id=1, source_target_pairs={{0,4},{1,17},{32,36},{33,49},{64,68},{65,81},{96,100},{97,113},{12... | collective-permute-start | bytes 786440 | tf_op jit(solution)/shard_map/ppermute | solution.py:337
  17.1 6.1 %collective-permute-start.2 = (bf16[256,512]{1,0:T(8,128)(2,1)S(1)}, bf16[256,512]{1,0:T(8,128)(2,1)S(1)}, u32[]{:S(2)}, u32[]{:S(2)}) collective-permute-start(bf16[256,512]{1,0:T(8,128)(2,1)S(1)} %get-tuple-element.11), channel_id=1, source_target_pairs={{0,2},{1,9},{32,34},{33,41},{64,66},{65,73},{96,98},{97,105},{128,... | collective-permute-start | bytes 786440 | tf_op jit(solution)/shard_map/ppermute | solution.py:337
  18.4 4.8 %collective-permute-start.3 = (bf16[256,512]{1,0:T(8,128)(2,1)S(1)}, bf16[256,512]{1,0:T(8,128)(2,1)S(1)}, u32[]{:S(2)}, u32[]{:S(2)}) collective-permute-start(bf16[256,512]{1,0:T(8,128)(2,1)S(1)} %get-tuple-element.10), channel_id=1, source_target_pairs={{0,6},{1,25},{32,38},{33,57},{64,70},{65,89},{96,102},{97,121},{12... | collective-permute-start | bytes 786440 | tf_op jit(solution)/shard_map/ppermute | solution.py:337
  23.5 4.8 %collective-permute-start.4 = (bf16[272,512]{1,0:T(8,128)(2,1)S(1)}, bf16[272,512]{1,0:T(8,128)(2,1)S(1)}, u32[]{:S(2)}, u32[]{:S(2)}) collective-permute-start(bf16[272,512]{1,0:T(8,128)(2,1)S(1)} %concatenate.4), channel_id=1, source_target_pairs={{0,16},{2,18},{4,20},{6,22},{1,5},{9,13},{17,21},{25,29},{32,48},{... | collective-permute-start | bytes 835592 | tf_op jit(solution)/shard_map/ppermute | solution.py:337
  24.8 6.4 %collective-permute-start.5 = (bf16[272,512]{1,0:T(8,128)(2,1)S(1)}, bf16[272,512]{1,0:T(8,128)(2,1)S(1)}, u32[]{:S(2)}, u32[]{:S(2)}) collective-permute-start(bf16[272,512]{1,0:T(8,128)(2,1)S(1)} %concatenate.4), channel_id=1, source_target_pairs={{0,8},{2,10},{4,12},{6,14},{1,3},{9,11},{17,19},{25,27},{32,40},{3... | collective-permute-start | bytes 835592 | tf_op jit(solution)/shard_map/ppermute | solution.py:337
  26.1 5.1 %collective-permute-start.6 = (bf16[272,512]{1,0:T(8,128)(2,1)S(1)}, bf16[272,512]{1,0:T(8,128)(2,1)S(1)}, u32[]{:S(2)}, u32[]{:S(2)}) collective-permute-start(bf16[272,512]{1,0:T(8,128)(2,1)S(1)} %concatenate.4), channel_id=1, source_target_pairs={{0,24},{2,26},{4,28},{6,30},{1,7},{9,15},{17,23},{25,31},{32,56},{... | collective-permute-start | bytes 835592 | tf_op jit(solution)/shard_map/ppermute | solution.py:337
  31.3 20.0 %copy-start.2 = (bf16[272,512]{1,0:T(8,128)(2,1)}, bf16[272,512]{1,0:T(8,128)(2,1)S(1)}, u32[]{:S(2)}) copy-start(bf16[272,512]{1,0:T(8,128)(2,1)S(1)} %add_select_fusion.refs_0_) | copy-start | bytes 835588
  31.4 7.9 %collective-permute-start.7 = (bf16[272,512]{1,0:T(8,128)(2,1)S(1)}, bf16[272,512]{1,0:T(8,128)(2,1)S(1)}, u32[]{:S(2)}, u32[]{:S(2)}) collective-permute-start(bf16[272,512]{1,0:T(8,128)(2,1)S(1)} %add_select_fusion.refs_0_), channel_id=1, source_target_pairs={{0,2},{2,4},{4,6},{6,0},{8,10},{10,12},{12,14},{14,8},{16,18},{18,... | collective-permute-start | bytes 835592 | tf_op jit(solution)/shard_map/ppermute | solution.py:337
  33.3 9.4 %collective-permute-start.8 = (bf16[272,512]{1,0:T(8,128)(2,1)S(1)}, bf16[272,512]{1,0:T(8,128)(2,1)S(1)}, u32[]{:S(2)}, u32[]{:S(2)}) collective-permute-start(bf16[272,512]{1,0:T(8,128)(2,1)S(1)} %add_select_fusion.refs_0_), channel_id=1, source_target_pairs={{0,4},{2,6},{4,0},{6,2},{8,12},{10,14},{12,8},{14,10},{16,20},{18,... | collective-permute-start | bytes 835592 | tf_op jit(solution)/shard_map/ppermute | solution.py:337
  35.5 10.3 %collective-permute-start.9 = (bf16[272,512]{1,0:T(8,128)(2,1)S(1)}, bf16[272,512]{1,0:T(8,128)(2,1)S(1)}, u32[]{:S(2)}, u32[]{:S(2)}) collective-permute-start(bf16[272,512]{1,0:T(8,128)(2,1)S(1)} %add_select_fusion.refs_0_), channel_id=1, source_target_pairs={{0,6},{2,0},{4,2},{6,4},{8,14},{10,8},{12,10},{14,12},{16,22},{18,... | collective-permute-start | bytes 835592 | tf_op jit(solution)/shard_map/ppermute | solution.py:337
  36.4 28.1 %collective-permute-start.10 = (bf16[272,512]{1,0:T(8,128)(2,1)S(1)}, bf16[272,512]{1,0:T(8,128)(2,1)S(1)}, u32[]{:S(2)}, u32[]{:S(2)}) collective-permute-start(bf16[272,512]{1,0:T(8,128)(2,1)S(1)} %add_select_fusion.refs_0_), channel_id=1, source_target_pairs={{0,1},{1,0},{2,3},{3,2},{4,5},{5,4},{6,7},{7,6},{8,9},{9,8},{10,11... | collective-permute-start | bytes 835592 | tf_op jit(solution)/shard_map/ppermute | solution.py:337
  39.2 12.1 %copy-start.4 = (bf16[272,512]{1,0:T(8,128)(2,1)}, bf16[272,512]{1,0:T(8,128)(2,1)S(1)}, u32[]{:S(2)}) copy-start(bf16[272,512]{1,0:T(8,128)(2,1)S(1)} %collective-permute-done.7.refs_1_) | copy-start | bytes 835588
  39.2 25.3 %collective-permute-start.11 = (bf16[272,512]{1,0:T(8,128)(2,1)S(1)}, bf16[272,512]{1,0:T(8,128)(2,1)S(1)}, u32[]{:S(2)}, u32[]{:S(2)}) collective-permute-start(bf16[272,512]{1,0:T(8,128)(2,1)S(1)} %collective-permute-done.7.refs_1_), channel_id=1, source_target_pairs={{0,1},{1,0},{2,3},{3,2},{4,5},{5,4},{6,7},{7,6},{8,9},{9,8},{10,11... | collective-permute-start | bytes 835592 | tf_op jit(solution)/shard_map/ppermute | solution.py:337
  42.8 8.6 %copy-start.5 = (bf16[272,512]{1,0:T(8,128)(2,1)}, bf16[272,512]{1,0:T(8,128)(2,1)S(1)}, u32[]{:S(2)}) copy-start(bf16[272,512]{1,0:T(8,128)(2,1)S(1)} %collective-permute-done.8.refs_2_) | copy-start | bytes 835588
  42.8 21.8 %collective-permute-start.12 = (bf16[272,512]{1,0:T(8,128)(2,1)S(1)}, bf16[272,512]{1,0:T(8,128)(2,1)S(1)}, u32[]{:S(2)}, u32[]{:S(2)}) collective-permute-start(bf16[272,512]{1,0:T(8,128)(2,1)S(1)} %collective-permute-done.8.refs_2_), channel_id=1, source_target_pairs={{0,1},{1,0},{2,3},{3,2},{4,5},{5,4},{6,7},{7,6},{8,9},{9,8},{10,11... | collective-permute-start | bytes 835592 | tf_op jit(solution)/shard_map/ppermute | solution.py:337
  45.8 5.5 %copy-start.6 = (bf16[272,512]{1,0:T(8,128)(2,1)}, bf16[272,512]{1,0:T(8,128)(2,1)S(1)}, u32[]{:S(2)}) copy-start(bf16[272,512]{1,0:T(8,128)(2,1)S(1)} %collective-permute-done.9.refs_3_) | copy-start | bytes 835588
  45.9 18.7 %collective-permute-start.13 = (bf16[272,512]{1,0:T(8,128)(2,1)S(1)}, bf16[272,512]{1,0:T(8,128)(2,1)S(1)}, u32[]{:S(2)}, u32[]{:S(2)}) collective-permute-start(bf16[272,512]{1,0:T(8,128)(2,1)S(1)} %collective-permute-done.9.refs_3_), channel_id=1, source_target_pairs={{0,1},{1,0},{2,3},{3,2},{4,5},{5,4},{6,7},{7,6},{8,9},{9,8},{10,11... | collective-permute-start | bytes 835592 | tf_op jit(solution)/shard_map/ppermute | solution.py:337
  64.5 0.7 copy-start.7
  64.5 0.8 copy-start.8
  64.5 0.9 copy-start.9
  64.5 1.0 copy-start.10
  103.5 23.8 %all-to-all-start.1 = ((f32[32,16,512]{2,1,0:T(8,128)}), f32[32,16,512]{2,1,0:T(8,128)S(1)}, u32[]{:S(2)}, u32[]{:S(2)}) async-start(f32[32,16,512]{2,1,0:T(8,128)} %broadcast_in_dim.13), calls=%async_computation.1 | async-start | bytes 2097152 | tf_op jit(solution)/shard_map/all_to_all | solution.py:399
  110.2 74.0 %all-reduce.2.cloned.1.call-start = ((), (), s32[]{:S(2)}) async-start(), calls=%async_computation.2 | async-start | bytes 3145728 | tf_op jit(solution)/shard_map/psum | solution.py:397
  127.3 1.0 copy-start.1
Sparse Core Ops, SparseCore 0:
  113.4 70.8 all-reduce.1
